TPU v7x, 512 devices: a whole 4x4x16 slice. The times are simulated.
512 devices in a mesh: center: 128 (over x, z, core), batch: 4 (over y).
Axes of the slice: x: 4, y: 4, z: 16, core: 2. Of those that a mesh axis runs over, the one named last changes fastest.
Arguments:
- centers: bfloat16 [65536, 384], P('center'), may hold values from -4 to 4
- weights: bfloat16 [65536, 512], P('center'), may hold values from -1 to 1
- subset_index: int32 [12288], P('center'), may hold values from 0 to 65535, as said below
- basis: bfloat16 [12288, 256], P('center'), may hold values from -2 to 2
- damping: float32 [256], replicated, may hold values from 0.2 to 0.95
- stored_train_features: bfloat16 [4, 8192, 384], P('batch', 'center'), may hold values from -4 to 4
- pool_labels: bfloat16 [4, 8192, 512], P('batch', 'center'), may hold values from -4 to 4
- picks: int32 [4, 256], P('batch', 'center'), may hold values from 0 to 63
Outputs:
- new_weights: bfloat16 [65536, 512], P('center')
- residual: bfloat16 [4, 256, 512], P('batch', 'center')
Inputs may be any that keep to these rules, and one draw needn't show every extreme that they name: `subset_index`: the entries are distinct centers; center p is held by index p // 512 of center. Of the 96 entries on one device at most 3 are held by any one index, and in every draw some index holds exactly 3 of the entries of every device.
All inputs are finite; a program needn't handle non-finite values.
Results may differ from a plain program's by a relative error of at most 0.013.
Values may be sent and summed in bfloat16 or wider, within the bound.
No kernel may reach another device: no remote copies, remote signals or barrier semaphores. Data moves between devices by JAX's collectives and lax.ppermute only.
A program may use at most 64 MiB of HBM per device.

v0:
```python
import jax
import jax.numpy as jnp
from jax import lax
from jax.sharding import PartitionSpec as P

kernel_length = 2.0
step_rate = 0.1


def per_device(
    centers, weights, subset_index, basis, damping, stored_train_features, pool_labels, picks
):
    devices = lax.axis_size("center")
    own_rows = picks.shape[1]
    center_rows = centers.shape[0]
    own_features = jnp.take(stored_train_features[0], picks[0], axis=0)
    own_targets = jnp.take(pool_labels[0], picks[0], axis=0)
    centers_sq = jnp.sum(jnp.square(centers.astype(jnp.float32)), axis=1)
    holder = subset_index // center_rows
    local_row = subset_index - holder * center_rows
    entries = subset_index.shape[0]
    capacity = 4 * entries // devices
    same_holder = holder[:, None] == holder[None, :]
    earlier = (
        jnp.arange(entries, dtype=jnp.int32)[:, None]
        > jnp.arange(entries, dtype=jnp.int32)[None, :]
    )
    slot_rank = jnp.sum((same_holder & earlier).astype(jnp.int32), axis=1)
    send_rows = (
        jnp.zeros((devices, capacity, basis.shape[1]), jnp.bfloat16)
        .at[holder, slot_rank]
        .set(basis)
    )
    send_local = jnp.zeros((devices, capacity), jnp.int32).at[holder, slot_rank].set(local_row)
    got_rows, got_local = (
        lax.all_to_all(send_rows, "center", split_axis=0, concat_axis=0, tiled=True),
        lax.all_to_all(send_local, "center", split_axis=0, concat_axis=0, tiled=True),
    )
    flattened_row_list = got_rows.reshape(devices * capacity, basis.shape[1])
    flat_local = got_local.reshape(devices * capacity)
    group_features, group_targets = (
        lax.all_gather(own_features, "center", axis=0, tiled=True),
        lax.all_gather(own_targets, "center", axis=0, tiled=True),
    )
    portion_sq = jnp.sum(jnp.square(group_features.astype(jnp.float32)), axis=1)
    cross = lax.dot_general(
        group_features, centers, (((1,), (1,)), ((), ())), preferred_element_type=jnp.float32
    )
    distance = portion_sq[:, None] + centers_sq[None, :] - 2.0 * cross
    laplace_kernel = jnp.exp(-jnp.sqrt(jnp.maximum(distance, 0.0)) / kernel_length).astype(
        jnp.bfloat16
    )
    predicted = lax.psum(
        jnp.dot(laplace_kernel, weights, preferred_element_type=jnp.float32), "center"
    )
    group_residual = (predicted - group_targets.astype(jnp.float32)).astype(jnp.bfloat16)
    residual = lax.dynamic_slice_in_dim(
        group_residual, lax.axis_index("center") * own_rows, own_rows, 0
    )
    group_grad = lax.dot_general(
        laplace_kernel, group_residual, (((0,), (0,)), ((), ())), preferred_element_type=jnp.float32
    )
    gradient = step_rate * lax.psum(group_grad.astype(jnp.bfloat16), "batch").astype(jnp.float32)
    picked = jnp.take(gradient, flat_local, axis=0).astype(jnp.bfloat16)
    partial_projection = lax.dot_general(
        flattened_row_list, picked, (((0,), (0,)), ((), ())), preferred_element_type=jnp.float32
    )
    projected = lax.psum(partial_projection, "center")
    scaled = (damping[:, None] * projected).astype(jnp.bfloat16)
    correction = jnp.dot(flattened_row_list, scaled, preferred_element_type=jnp.float32)
    updated = (weights.astype(jnp.float32) - gradient).at[flat_local].add(correction)
    return (updated.astype(jnp.bfloat16), residual[None])


def solution(mesh):
    return jax.shard_map(
        per_device,
        mesh=mesh,
        in_specs=(
            P("center", None),
            P("center", None),
            P("center"),
            P("center", None),
            P(),
            P("batch", "center", None),
            P("batch", "center", None),
            P("batch", "center"),
        ),
        out_specs=(P("center", None), P("batch", "center", None)),
        check_vma=False,
    )
```

profile of v0, /device:TPU:1, one launch (start us, length us, event | category | flops | bytes accessed | tf_op | source)
XLA Modules:
  0.0 879.9 jit_solution(11531714878231686000)
XLA Ops:
  8.1 4.9 scatter_fusion
  13.0 0.7 copy.15
  13.7 20.5 %all-to-all-start = ((s32[128,1,3]{2,1,0:T(1,128)}), s32[128,1,3]{2,1,0:T(1,128)S(1)}, u32[]{:S(2)}, u32[]{:S(2)}) async-start(s32[128,1,3]{2,1,0:T(1,128)} %copy.15), calls=%async_computation | async-start | bytes 131072 | tf_op jit(solution)/shard_map/all_to_all | solution.py:37
  34.5 1.4 gather_fusion
  36.0 99.5 %all-gather = bf16[128,2,384]{2,1,0:T(2,128)(2,1)S(1)} all-gather(bf16[1,2,384]{2,1,0:T(2,128)(2,1)S(1)} %fusion.15), channel_id=1, replica_groups=mesh['center'=128,'batch'=4] {'center'}, dimensions={0}, use_global_device_ids=true | all-gather | bytes 198144 | tf_op jit(solution)/shard_map/all_gather | solution.py:42
  136.7 1.1 fusion.21
  138.4 97.9 %all-gather.1 = bf16[128,2,512]{2,1,0:T(2,128)(2,1)S(1)} all-gather(bf16[1,2,512]{2,1,0:T(2,128)(2,1)S(1)} %fusion.13), channel_id=1, replica_groups=mesh['center'=128,'batch'=4] {'center'}, dimensions={0}, use_global_device_ids=true | all-gather | bytes 264192 | tf_op jit(solution)/shard_map/all_gather | solution.py:43
  236.4 0.8 copy-done.4
  237.1 5.5 scatter_fusion.1
  242.6 0.9 copy.16
  243.6 9.6 %all-to-all-start.1 = ((bf16[128,3,256]{2,1,0:T(4,128)(2,1)}), bf16[128,3,256]{2,1,0:T(4,128)(2,1)S(1)}, u32[]{:S(2)}, u32[]{:S(2)}) async-start(bf16[128,3,256]{2,1,0:T(4,128)(2,1)} %copy.16), calls=%async_computation.1 | async-start | bytes 524288 | tf_op jit(solution)/shard_map/all_to_all | solution.py:36
  254.0 0.8 reduce.7
  255.0 212.4 %all-reduce.4.cloned.1.call-done = f32[256,512]{1,0:T(8,128)} async-done(((f32[256,512]{1,0:T(8,128)}), f32[256,512]{1,0:T(8,128)}) %all-reduce.4.cloned.1.call-update) | async-done | bytes 524304 | tf_op jit(solution)/shard_map/psum | solution.py:53
  467.4 1.1 subtract_convert_fusion
  468.6 1.1 convolution_convert_fusion
  470.6 53.9 %all-reduce.6.cloned.1.call-done = bf16[512,512]{1,0:T(8,128)(2,1)} async-done(((bf16[512,512]{1,0:T(8,128)(2,1)}), bf16[512,512]{1,0:T(8,128)(2,1)}) %all-reduce.6.cloned.1.call-update) | async-done | bytes 524304 | tf_op jit(solution)/shard_map/psum | solution.py:63
  524.5 1.1 convert_multiply_fusion
  525.7 2.1 gather_fusion.2
  527.7 1.2 fusion.7
  528.9 1.0 copy-done.2
  530.1 337.6 %all-reduce.8.cloned.1.call-done = f32[256,512]{1,0:T(8,128)} async-done(((f32[256,512]{1,0:T(8,128)}), f32[256,512]{1,0:T(8,128)}) %all-reduce.8.cloned.1.call-update) | async-done | bytes 524304 | tf_op jit(solution)/shard_map/psum | solution.py:68
  867.7 1.4 fusion.10
  869.1 3.5 scatter_fusion.2
  872.5 0.9 convert_element_type.47
  (45 shorter events, 5.1 us)
Async XLA Ops:
  7.2 130.6 %copy-start = (bf16[1,64,512]{2,1,0:T(8,128)(2,1)S(1)}, bf16[1,64,512]{2,1,0:T(8,128)(2,1)}, u32[]{:S(2)}) copy-start(bf16[1,64,512]{2,1,0:T(8,128)(2,1)} %param.14) | copy-start | bytes 196612
  8.1 26.3 %copy-start.3 = (bf16[512,384]{1,0:T(8,128)(2,1)S(1)}, bf16[512,384]{1,0:T(8,128)(2,1)}, u32[]{:S(2)}) copy-start(bf16[512,384]{1,0:T(8,128)(2,1)} %param.8) | copy-start | bytes 1179652
  13.7 20.6 %copy-start.6 = (s32[1,2]{1,0:T(1,128)S(1)}, s32[1,2]{1,0:T(1,128)}, u32[]{:S(2)}) copy-start(s32[1,2]{1,0:T(1,128)} %param.15) | copy-start | bytes 28
  13.7 229.9 %all-to-all-start = ((s32[128,1,3]{2,1,0:T(1,128)}), s32[128,1,3]{2,1,0:T(1,128)S(1)}, u32[]{:S(2)}, u32[]{:S(2)}) async-start(s32[128,1,3]{2,1,0:T(1,128)} %copy.15), calls=%async_computation | async-start | bytes 131072 | tf_op jit(solution)/shard_map/all_to_all | solution.py:37
  34.3 433.2 %all-reduce.4.cloned.1.call-start = ((), (), s32[]{:S(2)}) async-start(), calls=%async_computation.2 | async-start | bytes 1048576 | tf_op jit(solution)/shard_map/psum | solution.py:53
  135.6 1.0 copy-start.1
  236.3 0.8 copy-start.4
  243.6 226.8 %all-to-all-start.1 = ((bf16[128,3,256]{2,1,0:T(4,128)(2,1)}), bf16[128,3,256]{2,1,0:T(4,128)(2,1)S(1)}, u32[]{:S(2)}, u32[]{:S(2)}) async-start(bf16[128,3,256]{2,1,0:T(4,128)(2,1)} %copy.16), calls=%async_computation.1 | async-start | bytes 524288 | tf_op jit(solution)/shard_map/all_to_all | solution.py:36
  253.2 271.3 %all-reduce.6.cloned.1.call-start = ((), (), s32[]{:S(2)}) async-start(), calls=%async_computation.3 | async-start | bytes 1048576 | tf_op jit(solution)/shard_map/psum | solution.py:63
  469.7 398.0 %all-reduce.8.cloned.1.call-start = ((), (), s32[]{:S(2)}) async-start(), calls=%async_computation.4 | async-start | bytes 1048576 | tf_op jit(solution)/shard_map/psum | solution.py:68
  528.9 1.0 copy-start.2
  530.0 337.7 %copy-start.5 = (f32[256]{0:T(256)S(1)}, f32[256]{0:T(256)}, u32[]{:S(2)}) copy-start(f32[256]{0:T(256)} %param.12) | copy-start | bytes 3076
Sparse Core Ops, SparseCore 0:
  137.9 329.4 all-reduce.3
  470.4 54.1 all-reduce.5
  529.1 338.5 all-reduce.7
where the time goes:
time: 880 us
  waiting for transfers between devices  604 us (69%)
  blocking collectives  197 us (22%)
  starting transfers between devices  30.3 us (3%)
  local copies, waits for them, and re-layouts  20.2 us (2%)
  between operations  14 us (2%)
  other arithmetic  8.91 us (1%)
    psum x1, waiting for transfers between devices, per_device(): projected = lax.psum(partial_projection, 'center')  338 us
    psum x1, waiting for transfers between devices, per_device(): lax.psum(jnp.dot(laplace_kernel, weights, preferred_element_type=jnp.floa...  212 us
    all_gather x1, blocking collectives, per_device(): lax.all_gather(own_features, 'center', axis=0, tiled=True)  99.5 us
    all_gather x1, blocking collectives, per_device(): lax.all_gather(own_targets, 'center', axis=0, tiled=True)  97.9 us
    psum x1, waiting for transfers between devices, per_device(): lax.psum(group_grad.astype(jnp.bfloat16), 'batch').astype(jnp.float32)  53.9 us
    all_to_all x1, starting transfers between devices, per_device(): lax.all_to_all(send_local, 'center', split_axis=0, concat_axis=0, tiled=T...  20.5 us
  transfers between devices with their start and end apart: 5, of which 3 were waited for; matrix products, arithmetic and copies ran while one was open for 2% of the time, Pallas kernels for 0%

commit v1 on v0

v1 whole, which is shorter than its diff:
```python
import jax
import jax.numpy as jnp
from jax import lax
from jax.sharding import Mesh, PartitionSpec as P

kernel_length = 2.0
step_rate = 0.1
f32 = jnp.float32
bf16 = jnp.bfloat16


def exchange(values, axes):
    return lax.all_to_all(values, axes, split_axis=0, concat_axis=0, tiled=True)


def rows_dot(left, right):
    return lax.dot_general(left, right, (((0,), (0,)), ((), ())), preferred_element_type=f32)


def laplace(features, centers, centers_sq):
    sample_sq = jnp.sum(jnp.square(features.astype(f32)), axis=1)
    cross = lax.dot_general(
        features, centers, (((1,), (1,)), ((), ())), preferred_element_type=f32
    )
    distance = sample_sq[:, None] + centers_sq[None, :] - 2.0 * cross
    return jnp.exp(-jnp.sqrt(jnp.maximum(distance, 0.0)) / kernel_length).astype(bf16)


def pick_row(stored, picks):
    lanes = lax.broadcasted_iota(jnp.int32, (picks.shape[0], stored.shape[0]), 1)
    return jnp.dot(
        (picks[:, None] == lanes).astype(bf16), stored, preferred_element_type=f32
    ).astype(bf16)


def per_device(
    centers, weights, subset_index, basis, damping, stored_train_features, pool_labels, picks
):
    nx, nz, nc, ny = (lax.axis_size(a) for a in ("x", "z", "core", "batch"))
    devices = nx * nz * nc
    own_rows = picks.shape[1]
    center_rows, width = centers.shape
    outputs = weights.shape[1]
    entries, eigen = basis.shape
    capacity = 4 * entries // devices
    block = nz * own_rows
    group = lax.axis_index("batch")
    core = lax.axis_index("core")

    own_features = pick_row(stored_train_features[0], picks[0])

    holder = subset_index // center_rows
    local_row = subset_index - holder * center_rows
    order = lax.iota(jnp.int32, entries)
    same_holder = holder[:, None] == holder[None, :]
    rank = jnp.sum((same_holder & (order[:, None] > order[None, :])).astype(jnp.int32), axis=1)
    lane = lax.broadcasted_iota(jnp.int32, (entries, eigen), 1)
    digit = jnp.where(lane % 2 == 0, (local_row % 256)[:, None], (local_row // 256)[:, None])
    position = jnp.where(lane // 2 == rank[:, None], digit, 0).astype(bf16)
    carried = jnp.where(
        group < capacity, jnp.where((rank == group)[:, None], basis, 0), position
    )
    column = holder // (nz * nc)
    spread = jnp.concatenate(
        [jnp.where((column == k)[:, None], carried, 0) for k in range(nx)], axis=1
    )
    goal = lax.broadcasted_iota(jnp.int32, (nz * nc, entries), 0)
    slots = jnp.dot(
        (goal == (holder % (nz * nc))[None, :]).astype(bf16), spread, preferred_element_type=f32
    ).astype(bf16)
    first = jnp.concatenate(
        [
            jnp.broadcast_to(own_features[None], (nz, own_rows, width)),
            slots.reshape(nz, nc, nx * eigen),
        ],
        axis=2,
    )
    first = exchange(first, "z").reshape(block, width + nx * eigen)
    second = jnp.stack(
        [
            jnp.concatenate(
                [first[:, :width], first[:, width + k * eigen : width + (k + 1) * eigen]], axis=1
            )
            for k in range(nx)
        ]
    )
    second = jnp.broadcast_to(second[None], (ny, nx, block, width + eigen))
    second = exchange(second.reshape(ny * nx, block, width + eigen), ("batch", "x"))
    features = lax.all_gather(second[:, :, :width], "core").reshape(nc, ny, nx * block, width)
    packed = lax.all_gather(second[:, :, width:], "core").reshape(nc, ny, nx * block, eigen)

    digits = packed[:, capacity].astype(f32)
    parity = lax.broadcasted_iota(jnp.int32, (nc, nx * block), 1) % nc
    places = jnp.stack(
        [
            jnp.where(
                parity == core, digits[:, :, 2 * k] + 256.0 * digits[:, :, 2 * k + 1], -1.0
            )
            for k in range(capacity)
        ],
        axis=1,
    ).astype(jnp.int32)
    places = places.reshape(nc * capacity * nx * block, 1)
    member = (
        places == lax.broadcasted_iota(jnp.int32, (places.shape[0], center_rows), 1)
    ).astype(bf16)
    local_basis = rows_dot(
        member, packed[:, :capacity].reshape(nc * capacity * nx * block, eigen)
    ).astype(bf16)

    centers_sq = jnp.sum(jnp.square(centers.astype(f32)), axis=1)
    own_group = lax.dynamic_index_in_dim(features, group, 1, keepdims=False)
    own_kernel = laplace(own_group.reshape(nc * nx * block, width), centers, centers_sq)
    partial = jnp.dot(
        own_kernel, jnp.concatenate([weights, local_basis], axis=1), preferred_element_type=f32
    ).astype(bf16)
    wide = outputs + eigen
    partial = exchange(partial.reshape(nc * nx, block, wide), ("core", "x"))
    partial = jnp.sum(partial.astype(f32), axis=0).astype(bf16)
    partial = exchange(partial.reshape(nz, own_rows, wide), "z")
    total = jnp.sum(partial.astype(f32), axis=0)
    own_targets = pick_row(pool_labels[0], picks[0])
    residual = (total[:, :outputs] - own_targets.astype(f32)).astype(bf16)
    own = jnp.concatenate([residual, total[:, outputs:].astype(bf16)], axis=1)

    own = exchange(jnp.broadcast_to(own[None], (nz, own_rows, wide)), "z")
    own = jnp.broadcast_to(own.reshape(1, block, wide), (ny * nx, block, wide))
    here = exchange(own, ("batch", "x")).reshape(ny * nx * block, wide)
    there = lax.ppermute(here, "core", [(k, nc - 1 - k) for k in range(nc)])

    features = features.reshape(nc, ny * nx * block, width)
    kernel_here = laplace(
        lax.dynamic_index_in_dim(features, core, 0, keepdims=False), centers, centers_sq
    )
    kernel_there = laplace(
        lax.dynamic_index_in_dim(features, nc - 1 - core, 0, keepdims=False), centers, centers_sq
    )
    projected = rows_dot(here[:, outputs:], here[:, :outputs]) + rows_dot(
        there[:, outputs:], there[:, :outputs]
    )
    scaled = (damping[:, None] * projected).astype(bf16)
    gradient = rows_dot(kernel_here, here[:, :outputs]) + rows_dot(
        kernel_there, there[:, :outputs]
    )
    change = gradient - jnp.dot(local_basis, scaled, preferred_element_type=f32)
    updated = (weights.astype(f32) - step_rate * change).astype(bf16)
    return (updated, residual[None])


def solution(mesh):
    devices = mesh.devices
    fine = Mesh(
        devices.reshape(4, devices.shape[0] // 8, 2, devices.shape[1]),
        ("x", "z", "core", "batch"),
    )
    center = ("x", "z", "core")
    return jax.shard_map(
        per_device,
        mesh=fine,
        in_specs=(
            P(center, None),
            P(center, None),
            P(center),
            P(center, None),
            P(),
            P("batch", center, None),
            P("batch", center, None),
            P("batch", center),
        ),
        out_specs=(P(center, None), P("batch", center, None)),
        check_vma=False,
    )
```

time: 880 us -> 130 us (0.15)
  waiting for transfers between devices: 604 us -> 10.3 us
  blocking collectives: 197 us -> 89.3 us
  local copies, waits for them, and re-layouts: 20.2 us -> 1.44 us
  starting transfers between devices: 30.3 us -> 13 us
  between operations: 14 us -> 1.01 us
    psum x3 -> x0, waiting for transfers between devices: 604 us -> none  [the longest x1 338 us: per_device(): projected = lax.psum(partial_projection, 'center')]
    all_gather x2, blocking collectives: 197 us -> 7.77 us  [the longest x1 5.27 us: per_device(): lax.all_gather(second[:, :, width:], 'core')]
    all_to_all x0 -> x5, blocking collectives: none -> 81.6 us  [exchange(): return lax.all_to_all(values, axes, split_axis=0, concat_axis=0, tiled=True)]
    all_to_all x2 -> x1, starting transfers between devices: 30.2 us -> 6.75 us  [exchange(): return lax.all_to_all(values, axes, split_axis=0, concat_axis=0, tiled=True)]
    scatter x3 -> x0, local copies, waits for them, and re-layouts: 11.3 us -> none  [the longest x2 6.36 us: per_device(): send_rows = jnp.zeros((devices, capacity, basis.shape[1]), jnp.bfloat16)....]
    all_to_all x2 -> x1, waiting for transfers between devices: 0.01 us -> 10.3 us  [exchange(): return lax.all_to_all(values, axes, split_axis=0, concat_axis=0, tiled=True)]
  transfers between devices with their start and end apart: 5 -> 2, of which waited for: 3 -> 1; matrix products, arithmetic and copies ran while one was open for 2% -> 2% of each run, Pallas kernels for 0% -> 0%
where the time goes in v1:
time: 130 us; the launch traced here: 129 us
  blocking collectives  89.3 us (69%)
  starting transfers between devices  13 us (10%)
  waiting for transfers between devices  10.3 us (8%)
  matrix products  9.47 us (7%)
  other arithmetic  4.46 us (3%)
  local copies, waits for them, and re-layouts  1.44 us (1%)
    all_to_all x5, blocking collectives, exchange(): return lax.all_to_all(values, axes, split_axis=0, concat_axis=0, tiled=True)  81.6 us
    all_to_all x1, waiting for transfers between devices, exchange(): return lax.all_to_all(values, axes, split_axis=0, concat_axis=0, tiled=True)  10.3 us
    all_to_all x1, starting transfers between devices, exchange(): return lax.all_to_all(values, axes, split_axis=0, concat_axis=0, tiled=True)  6.75 us
    dot_general x4, matrix products, rows_dot(): lax.dot_general(left, right, (((0,), (0,)), ((), ())), preferred_element_...  6.46 us
    ppermute x1, starting transfers between devices, per_device(): there = lax.ppermute(here, 'core', [(k, nc - 1 - k) for k in range(nc)])  6.28 us
    all_gather x1, blocking collectives, per_device(): lax.all_gather(second[:, :, width:], 'core')  5.27 us
  transfers between devices with their start and end apart: 2, of which 1 were waited for; matrix products, arithmetic and copies ran while one was open for 2% of the time, Pallas kernels for 0%

profile of v1, /device:TPU:1, one launch (start us, length us, event | category | flops | bytes accessed | tf_op | source)
XLA Modules:
  0.0 129.1 jit_solution(10083655189441459203)
XLA Ops:
  0.7 0.7 and_select_fusion.3
  1.6 0.7 and_select_fusion.1
  2.3 0.7 and_select_fusion
  3.0 0.9 broadcast_select_fusion.3
  4.5 27.3 %all_to_all.30 = bf16[16,2,1408]{2,1,0:T(2,128)(2,1)S(1)} all-to-all(bf16[16,2,1408]{2,1,0:T(2,128)(2,1)S(1)} %pad_maximum_fusion.1), channel_id=1, replica_groups=mesh['x'=4,'z'=16,'core'=2,'batch'=4] {'z'}, dimensions={0} | all-to-all | bytes 180224 | tf_op jit(solution)/shard_map/all_to_all | solution.py:13
  32.0 0.9 broadcast_in_dim.117
  32.9 6.8 %all-to-all-start.1 = ((bf16[16,32,640]{2,1,0:T(8,128)(2,1)}), bf16[16,32,640]{2,1,0:T(8,128)(2,1)S(1)}, u32[]{:S(2)}, u32[]{:S(2)}) async-start(bf16[16,32,640]{2,1,0:T(8,128)(2,1)} %bitcast.6), calls=%async_computation.1 | async-start | bytes 1310720 | tf_op jit(solution)/shard_map/all_to_all | solution.py:13
  39.9 10.3 %all-to-all-done.1 = bf16[16,32,640]{2,1,0:T(8,128)(2,1)S(1)} async-done(((bf16[16,32,640]{2,1,0:T(8,128)(2,1)}), bf16[16,32,640]{2,1,0:T(8,128)(2,1)S(1)}, u32[]{:S(2)}, u32[]{:S(2)}) %all-to-all-start.1) | async-done | bytes 655392 | tf_op jit(solution)/shard_map/all_to_all | solution.py:13
  50.2 5.3 %all-gather.1 = bf16[32,32,256]{2,1,0:T(8,128)(2,1)S(1)} all-gather(bf16[16,32,256]{2,1,0:T(8,128)(2,1)S(1)} %slice.93), channel_id=3, replica_groups=mesh['x'=4,'z'=16,'core'=2,'batch'=4] {'core'}, dimensions={0}, use_global_device_ids=true | all-gather | bytes 786432 | tf_op jit(solution)/shard_map/all_gather | solution.py:90
  55.5 0.4 fusion.86
  56.0 0.6 fusion.28
  56.7 2.5 %all-gather = bf16[32,32,384]{2,1,0:T(8,128)(2,1)S(1)} all-gather(bf16[16,32,384]{2,1,0:T(8,128)(2,1)S(1)} %slice.92), channel_id=2, replica_groups=mesh['x'=4,'z'=16,'core'=2,'batch'=4] {'core'}, dimensions={0}, use_global_device_ids=true | all-gather | bytes 1179648 | tf_op jit(solution)/shard_map/all_gather | solution.py:89
  59.4 0.7 convolution_convert_fusion
  60.1 10.8 %all_to_all.31 = bf16[8,32,768]{2,1,0:T(8,128)(2,1)S(1)} all-to-all(bf16[8,32,768]{2,1,0:T(8,128)(2,1)S(1)} %bitcast.62), channel_id=1, replica_groups=mesh['x'=4,'z'=16,'core'=2,'batch'=4] {'core','x'}, dimensions={0} | all-to-all | bytes 786432 | tf_op jit(solution)/shard_map/all_to_all | solution.py:13
  70.9 15.8 %all_to_all.32 = bf16[16,2,768]{2,1,0:T(2,128)(2,1)S(1)} all-to-all(bf16[16,2,768]{2,1,0:T(2,128)(2,1)S(1)} %reshape.320), channel_id=1, replica_groups=mesh['x'=4,'z'=16,'core'=2,'batch'=4] {'z'}, dimensions={0} | all-to-all | bytes 98304 | tf_op jit(solution)/shard_map/all_to_all | solution.py:13
  86.8 0.2 fusion.33
  87.1 14.0 %all_to_all.33 = bf16[16,2,768]{2,1,0:T(2,128)(2,1)S(1)} all-to-all(bf16[16,2,768]{2,1,0:T(2,128)(2,1)S(1)} %broadcast_in_dim.119), channel_id=1, replica_groups=mesh['x'=4,'z'=16,'core'=2,'batch'=4] {'z'}, dimensions={0} | all-to-all | bytes 98304 | tf_op jit(solution)/shard_map/all_to_all | solution.py:13
  101.2 13.6 %all_to_all.34 = bf16[16,32,768]{2,1,0:T(8,128)(2,1)S(1)} all-to-all(bf16[16,32,768]{2,1,0:T(8,128)(2,1)S(1)} %broadcast_in_dim.121), channel_id=1, replica_groups=mesh['x'=4,'z'=16,'core'=2,'batch'=4] {'batch','x'}, dimensions={0} | all-to-all | bytes 1572864 | tf_op jit(solution)/shard_map/all_to_all | solution.py:13
  114.8 6.3 %collective-permute-start = (bf16[512,768]{1,0:T(8,128)(2,1)S(1)}, bf16[512,768]{1,0:T(8,128)(2,1)}, u32[]{:S(2)}, u32[]{:S(2)}) collective-permute-start(bf16[512,768]{1,0:T(8,128)(2,1)S(1)} %bitcast.56), channel_id=1, source_target_pairs={{0,4},{4,0},{1,5},{5,1},{2,6},{6,2},{3,7},{7,3},{8,12},{12,8},{9,1... | collective-permute-start | bytes 2359304 | tf_op jit(solution)/shard_map/ppermute | solution.py:129
  121.1 0.2 multiply_reduce_fusion
  121.3 0.3 fusion.54
  121.7 2.1 %fusion.19 = f32[512,512]{1,0:T(8,128)} fusion(bf16[512,384]{1,0:T(8,128)(2,1)S(1)} %copy-done.1, f32[512]{0:T(512)S(1)} %multiply_reduce_fusion.1, f32[512]{0:T(512)S(1)} %get-tuple-element.3, bf16[512,768]{1,0:T(8,128)(2,1)S(1)} %bitcast.58, bf16[2,512,384]{2,1,0:T(8,128)(2,1)S(1)} %bitcast.54, s32[]{:T(128)S(6)} %select_n.144), kind=kOutput, calls=%fused_computation.24 | convolution fusion | flops 471597056 | bytes 2363396 | tf_op jit(solution)/shard_map/dot_general | solution.py:17
  123.8 1.8 %fusion.30 = f32[512,512]{1,0:T(8,128)S(1)} fusion(bf16[512,256]{0,1:T(8,128)(2,1)S(1)} %fusion.28, f32[256,512]{1,0:T(8,128)S(1)} %fusion.54, bf16[512,768]{1,0:T(8,128)(2,1)} %collective-permute-done, f32[256]{0:T(256)S(1)} %copy-done.4), kind=kOutput, calls=%fused_computation.37 | convolution fusion | flops 268828672 | bytes 2622464 | tf_op jit(solution)/shard_map/dot_general | solution.py:145
  125.6 3.5 %fusion.18 = bf16[512,512]{1,0:T(8,128)(2,1)} fusion(f32[512,512]{1,0:T(8,128)S(1)} %fusion.30, f32[512,512]{1,0:T(8,128)} %fusion.19, bf16[512,384]{1,0:T(8,128)(2,1)S(1)} %copy-done.2, bf16[512,512]{1,0:T(8,128)(2,1)} %param.9, f32[512]{0:T(512)S(1)} %get-tuple-element.2, f32[512]{0:T(512)S(1)} %multiply_reduce_fusion.1, ...), kind=kOutput, calls=%fused_computation.22 | convolution fusion | flops 473169920 | bytes 4460548 | tf_op jit(solution)/shard_map/dot_general | solution.py:17
  (57 shorter events, 1.7 us)
Async XLA Ops:
  0.6 86.2 %copy-start = (bf16[1,64,512]{2,1,0:T(8,128)(2,1)S(1)}, bf16[1,64,512]{2,1,0:T(8,128)(2,1)}, u32[]{:S(2)}) copy-start(bf16[1,64,512]{2,1,0:T(8,128)(2,1)} %param.14) | copy-start | bytes 196612
  0.6 3.6 %copy-start.7 = (s32[1,2]{1,0:T(1,128)S(1)}, s32[1,2]{1,0:T(1,128)}, u32[]{:S(2)}) copy-start(s32[1,2]{1,0:T(1,128)} %param.15) | copy-start | bytes 28
  0.7 3.6 %copy-start.6 = (bf16[1,64,384]{2,1,0:T(8,128)(2,1)S(1)}, bf16[1,64,384]{2,1,0:T(8,128)(2,1)}, u32[]{:S(2)}) copy-start(bf16[1,64,384]{2,1,0:T(8,128)(2,1)} %param.13) | copy-start | bytes 147460
  32.0 7.7 %copy-start.1 = (bf16[512,384]{1,0:T(8,128)(2,1)S(1)}, bf16[512,384]{1,0:T(8,128)(2,1)}, u32[]{:S(2)}) copy-start(bf16[512,384]{1,0:T(8,128)(2,1)} %param.8) | copy-start | bytes 1179652
  32.9 17.2 %all-to-all-start.1 = ((bf16[16,32,640]{2,1,0:T(8,128)(2,1)}), bf16[16,32,640]{2,1,0:T(8,128)(2,1)S(1)}, u32[]{:S(2)}, u32[]{:S(2)}) async-start(bf16[16,32,640]{2,1,0:T(8,128)(2,1)} %bitcast.6), calls=%async_computation.1 | async-start | bytes 1310720 | tf_op jit(solution)/shard_map/all_to_all | solution.py:13
  56.7 2.7 %copy-start.5 = (bf16[512,512]{1,0:T(8,128)(2,1)S(1)}, bf16[512,512]{1,0:T(8,128)(2,1)}, u32[]{:S(2)}) copy-start(bf16[512,512]{1,0:T(8,128)(2,1)} %param.9) | copy-start | bytes 1572868
  87.0 27.8 %copy-start.3 = (bf16[2,512]{1,0:T(2,128)(2,1)}, bf16[2,512]{1,0:T(2,128)(2,1)S(1)}, u32[]{:S(2)}) copy-start(bf16[2,512]{1,0:T(2,128)(2,1)S(1)} %fusion.33) | copy-start | bytes 6148
  114.8 9.0 %collective-permute-start = (bf16[512,768]{1,0:T(8,128)(2,1)S(1)}, bf16[512,768]{1,0:T(8,128)(2,1)}, u32[]{:S(2)}, u32[]{:S(2)}) collective-permute-start(bf16[512,768]{1,0:T(8,128)(2,1)S(1)} %bitcast.56), channel_id=1, source_target_pairs={{0,4},{4,0},{1,5},{5,1},{2,6},{6,2},{3,7},{7,3},{8,12},{12,8},{9,1... | collective-permute-start | bytes 2359304 | tf_op jit(solution)/shard_map/ppermute | solution.py:129
  121.7 2.1 %copy-start.4 = (f32[256]{0:T(256)S(1)}, f32[256]{0:T(256)}, u32[]{:S(2)}) copy-start(f32[256]{0:T(256)} %param.12) | copy-start | bytes 3076
  123.8 1.8 %copy-start.2 = (bf16[512,384]{1,0:T(8,128)(2,1)S(1)}, bf16[512,384]{1,0:T(8,128)(2,1)}, u32[]{:S(2)}) copy-start(bf16[512,384]{1,0:T(8,128)(2,1)} %param.8) | copy-start | bytes 1179652

commit v2 on v1

v2 whole, which is shorter than its diff:
```python
import functools

import jax
import jax.numpy as jnp
from jax import lax
from jax.experimental import pallas as pl
from jax.experimental.pallas import tpu as pltpu
from jax.sharding import Mesh, PartitionSpec as P

kernel_length = 2.0
step_rate = 0.1
f32 = jnp.float32
bf16 = jnp.bfloat16
i32 = jnp.int32
VMEM = pltpu.VMEM


def exchange(values, axes):
    return lax.all_to_all(values, axes, split_axis=0, concat_axis=0, tiled=True)


def iota(shape, dim):
    return lax.broadcasted_iota(i32, shape, dim)


def mxu(left, right, contract=((1,), (0,))):
    return lax.dot_general(left, right, (contract, ((), ())), preferred_element_type=f32)


def rows_dot(left, right):
    return mxu(left, right, ((0,), (0,)))


def laplace(distance):
    return jnp.exp(-jnp.sqrt(jnp.maximum(distance, 0.0)) / kernel_length).astype(bf16)


def prepare(sizes, *refs):
    nx, nz, nc, rows_each, capacity = sizes
    out_ref, target_ref = refs[5:7]
    picks_ref, index_ref, basis_ref, stored_ref, label_ref, done = refs[7:]
    copies = [
        pltpu.make_async_copy(source, target, done.at[k])
        for k, (source, target) in enumerate(zip(refs[:5], refs[7:12]))
    ]
    for copy in copies:
        copy.start()
    for copy in copies:
        copy.wait()
    entries, eigen = basis_ref.shape
    group = lax.axis_index("batch")
    upper = jnp.where(lax.axis_index("x") < nx // 2, 0, eigen // 8)
    half = eigen // 2
    depth, width = stored_ref.shape
    index = index_ref[...]
    eye = iota((entries, entries), 0) == iota((entries, entries), 1)
    bits = rows_each.bit_length() - 1
    holder = lax.shift_right_logical(index, bits)
    column = jnp.sum(jnp.where(eye, index, 0), axis=1, keepdims=True)
    column_holder = lax.shift_right_logical(column, bits)
    column_row = lax.bitwise_and(column, rows_each - 1)
    earlier = iota((entries, entries), 0) > iota((entries, entries), 1)
    rank = jnp.sum(
        jnp.where((column_holder == holder) & earlier, 1, 0), axis=1, keepdims=True
    )
    lane = lax.bitwise_and(iota((entries, eigen), 1), half - 1)
    low = lax.bitwise_and(column_row, 255)
    high = lax.shift_right_logical(column_row, 8)
    digit = jnp.where(lax.bitwise_and(lane, 1) == 0, low, high)
    position = jnp.where(lax.shift_right_logical(lane, 1) == rank + upper, digit, 0).astype(f32)
    kept = jnp.where(rank == group, basis_ref[...].astype(f32), 0.0)
    carried = jnp.where(group < capacity, kept, position)
    carried = jnp.concatenate([carried[:, :half], carried[:, half:]], axis=0)
    line_bits = (nz * nc).bit_length() - 1
    corner = lax.shift_right_logical(column_holder, line_bits) * nc + lax.bitwise_and(
        column_holder, nc - 1
    )
    corner = jnp.concatenate([corner, corner], axis=0)
    line = lax.shift_right_logical(lax.bitwise_and(holder, nz * nc - 1), nc.bit_length() - 1)
    here = iota((2 * nz, entries), 0)
    same = lax.shift_right_logical(here, 1) == line
    odd = lax.bitwise_and(here, 1)
    goal = jnp.concatenate(
        [jnp.where(same & (odd == h), 1.0, 0.0).astype(bf16) for h in range(2)], axis=1
    )
    sample = iota((2 * nz, depth), 0)
    wanted = jnp.where(lax.bitwise_and(sample, 1) == 0, picks_ref[0, 0], picks_ref[0, 1])
    picked = jnp.where(wanted == iota((2 * nz, depth), 1), 1.0, 0.0).astype(bf16)
    out_ref[:, :width] = mxu(picked, stored_ref[...]).astype(bf16)
    target_ref[...] = mxu(picked[: target_ref.shape[0], :], label_ref[...])
    for k in range(nx * nc):
        spread = jnp.where(corner == k, carried, 0.0).astype(bf16)
        out_ref[:, width + k * half : width + (k + 1) * half] = mxu(goal, spread).astype(bf16)


def squares(values):
    wide = values.astype(f32)
    return jnp.sum(wide * wide, axis=1, keepdims=True)


def as_row(column):
    return jnp.broadcast_to(column, (column.shape[0], 128)).T[:1, :]


def predict(sizes, place_ref, features_ref, kept_ref, pair_ref, centers_ref, weights_ref, *outs):
    nc, ny, capacity = sizes
    out_ref, basis_ref = outs
    core, group = place_ref[0], place_ref[1]
    other = nc - 1 - core
    count, width = features_ref.shape
    rows = centers_ref.shape[0]
    outputs = weights_ref.shape[1]
    side = count // ny
    parts = width // 128
    centers = centers_ref[...]
    line = as_row(squares(centers))

    def across(features):
        cross = mxu(features, centers, ((1,), (1,)))
        return laplace(squares(features) + line - 2.0 * cross)

    start = pl.multiple_of(group * side, side)
    near = across(features_ref[pl.ds(start, side), :])
    far = across(
        jnp.concatenate(
            [
                pair_ref[other, pl.ds(pl.multiple_of(k * count + start, side), side), :]
                for k in range(parts)
            ],
            axis=1,
        )
    )

    at = iota((rows, side), 0)
    parity = lax.bitwise_and(iota((1, side), 1), 1)
    halves = [jnp.zeros((rows, 128), f32) for _ in range(2)]
    for c in range(2):
        if c == 0:
            blocks = [kept_ref[k * side : (k + 1) * side, :] for k in range(capacity)]
            digits = kept_ref[capacity * side :, :]
        else:
            first = parts * count
            blocks = [
                pair_ref[other, first + k * side : first + (k + 1) * side, :]
                for k in range(capacity)
            ]
            digits = pair_ref[other, first + capacity * side :, :]
        digits = digits.astype(f32)
        digits = jnp.concatenate([digits, digits], axis=0).T
        for k in range(capacity):
            low, high = (
                digits[2 * k + d : 2 * k + d + 1, :] + 256.0 * digits[2 * k + d + 1 : 2 * k + d + 2, :]
                for d in (0, 64)
            )
            place = jnp.where(iota((1, side), 1) < side // 2, low, high).astype(i32)
            for h in range(2):
                held = jnp.where(parity == h, place, -1)
                member = jnp.where(at == held, 1.0, 0.0).astype(bf16)
                halves[h] = halves[h] + mxu(member, blocks[k])
    local = jnp.concatenate(halves, axis=1).astype(bf16)
    basis_ref[...] = local
    for kernel, to in ((near, core), (far, other)):
        spot = pl.ds(pl.multiple_of(to * side, side), side)
        out_ref[spot, :outputs] = mxu(kernel, weights_ref[...]).astype(bf16)
        out_ref[spot, outputs:] = mxu(kernel, local).astype(bf16)


def spread(place_ref, features_ref, pair_ref, centers_ref, here_ref, there_ref):
    other = 1 - place_ref[0]
    count, width = features_ref.shape
    centers = centers_ref[...]
    column = squares(centers)
    theirs = jnp.concatenate(
        [pair_ref[other, k * count : (k + 1) * count, :] for k in range(width // 128)], axis=1
    )
    for out_ref, features in ((here_ref, features_ref[...]), (there_ref, theirs)):
        cross = mxu(centers, features, ((1,), (1,)))
        out_ref[...] = laplace(column + as_row(squares(features)) - 2.0 * cross)


def begin(kernel_hbm, damping_hbm, here_ref, *refs):
    slope_ref, project_ref, column_ref, kernel_ref, damping_ref, done = refs
    outputs = slope_ref.shape[1]
    copies = [
        pltpu.make_async_copy(kernel_hbm, kernel_ref, done.at[0]),
        pltpu.make_async_copy(damping_hbm, damping_ref, done.at[1]),
    ]
    for copy in copies:
        copy.start()
    project_ref[...] = rows_dot(here_ref[:, outputs:], here_ref[:, :outputs])
    for copy in copies:
        copy.wait()
    slope_ref[...] = mxu(kernel_ref[...], here_ref[:, :outputs])
    row = damping_ref[...]
    column_ref[...] = jnp.broadcast_to(row, (128, row.shape[1])).T[:, :1]


def update(steps, kernel_ref, there_ref, slope_ref, project_ref, basis_ref, damping_ref, weights_ref, out_hbm, held, done):
    rows, outputs = weights_ref.shape
    total = project_ref[...] + rows_dot(there_ref[:, outputs:], there_ref[:, :outputs])
    scaled = (damping_ref[...] * total).astype(bf16)
    tall = rows // steps
    copies = []
    for k in range(steps):
        at = slice(k * tall, (k + 1) * tall)
        change = slope_ref[at, :] + mxu(kernel_ref[at, :], there_ref[:, :outputs])
        change = change - mxu(basis_ref[at, :], scaled)
        held[at, :] = (weights_ref[at, :].astype(f32) - step_rate * change).astype(bf16)
        copy = pltpu.make_async_copy(held.at[at, :], out_hbm.at[at, :], done.at[k])
        copy.start()
        copies.append(copy)
    for copy in copies:
        copy.wait()


def per_device(
    centers, weights, subset_index, basis, damping, stored_train_features, pool_labels, picks
):
    nx, nz, nc, ny = (lax.axis_size(a) for a in ("x", "z", "core", "batch"))
    devices = nx * nz * nc
    own_rows = picks.shape[1]
    center_rows, width = centers.shape
    outputs = weights.shape[1]
    entries, eigen = basis.shape
    capacity = 4 * entries // devices
    block = nz * own_rows
    side = nx * block
    wide = outputs + eigen
    half = eigen // 2
    group = lax.axis_index("batch")
    core = lax.axis_index("core")
    smem = pl.BlockSpec(memory_space=pltpu.SMEM)
    vmem = pl.BlockSpec(memory_space=VMEM)
    hbm = pl.BlockSpec(memory_space=pltpu.HBM)
    small = pltpu.CompilerParams(vmem_limit_bytes=16 * 1024 * 1024)

    first, own_targets = pl.pallas_call(
        functools.partial(prepare, (nx, nz, nc, center_rows, capacity)),
        out_shape=(
            jax.ShapeDtypeStruct((block, width + nx * eigen), bf16),
            jax.ShapeDtypeStruct((min(8, block), outputs), f32),
        ),
        in_specs=[hbm] * 5,
        out_specs=(vmem, vmem),
        scratch_shapes=[
            pltpu.SMEM((1, own_rows), i32),
            VMEM((1, entries), i32),
            VMEM((entries, eigen), bf16),
            VMEM(stored_train_features.shape[1:], bf16),
            VMEM(pool_labels.shape[1:], bf16),
            pltpu.SemaphoreType.DMA((5,)),
        ],
        compiler_params=small,
    )(
        *(
            pltpu.with_memory_space_constraint(v, pltpu.HBM)
            for v in (
                picks,
                subset_index.reshape(1, entries),
                basis,
                stored_train_features[0],
                pool_labels[0],
            )
        )
    )
    first = first.reshape(nz, own_rows, width + nx * eigen)
    first, group, core = lax.optimization_barrier((first, group, core))
    first = exchange(first, "z").reshape(block, width + nx * eigen)
    second = jnp.stack(
        [
            jnp.concatenate(
                [first[:, :width], first[:, width + k * eigen : width + (k + 1) * eigen]], axis=1
            )
            for k in range(nx)
        ]
    )
    second = jnp.broadcast_to(second[None], (ny, nx, block, width + eigen))
    second, group, core = lax.optimization_barrier((second, group, core))
    second = exchange(second.reshape(ny * nx, block, width + eigen), ("batch", "x"))
    second, group, core = lax.optimization_barrier((second, group, core))
    features = second[:, :, :width].reshape(ny * side, width)
    near = second[:, :, width : width + half].reshape(ny * side, half)
    far = second[:, :, width + half :].reshape(ny * side, half)
    kept, sent = jnp.where(core == 0, near, far), jnp.where(core == 0, far, near)
    places = capacity * side
    kept, sent = (
        jnp.concatenate([v[:places], v[places : places + side // 2] + v[places + side // 2 :]])
        for v in (kept, sent)
    )
    pair = lax.all_gather(
        jnp.concatenate(
            [features[:, k : k + 128] for k in range(0, width, 128)] + [sent], axis=0
        ),
        "core",
    )
    place = jnp.stack([core, group])
    partial, local_basis = pl.pallas_call(
        functools.partial(predict, (nc, ny, capacity)),
        out_shape=(
            jax.ShapeDtypeStruct((nc * side, wide), bf16),
            jax.ShapeDtypeStruct((center_rows, eigen), bf16),
        ),
        in_specs=[smem, vmem, vmem, vmem, vmem, vmem],
        out_specs=(vmem, vmem),
        compiler_params=small,
    )(place, features, kept, pair, centers, weights)
    partial = exchange(partial.reshape(nc * nx, block, wide), ("core", "x"))
    partial = jnp.sum(partial.astype(f32), axis=0).astype(bf16)
    partial, place = lax.optimization_barrier((partial, place))
    partial = exchange(partial.reshape(nz, own_rows, wide), "z")
    square = jax.ShapeDtypeStruct((center_rows, ny * side), bf16)
    kernel_here, kernel_there = pl.pallas_call(
        spread,
        out_shape=(square, square),
        in_specs=[smem, vmem, vmem, vmem],
        out_specs=(vmem, vmem),
        compiler_params=small,
    )(place, features, pair, centers)
    total = jnp.sum(partial.astype(f32), axis=0)
    residual = (total[:, :outputs] - own_targets[:own_rows]).astype(bf16)
    own = jnp.concatenate([residual, total[:, outputs:].astype(bf16)], axis=1)
    own, kernel_here, kernel_there = lax.optimization_barrier((own, kernel_here, kernel_there))

    own_all = exchange(jnp.broadcast_to(own[None], (nz, own_rows, wide)), "z")
    own_all = jnp.broadcast_to(own_all.reshape(1, block, wide), (ny * nx, block, wide))
    here = exchange(own_all, ("batch", "x"))
    residual = lax.dynamic_slice(
        here,
        (group * nx + lax.axis_index("x"), lax.axis_index("z") * own_rows, 0),
        (1, own_rows, outputs),
    )
    here = here.reshape(ny * side, wide)
    there = lax.ppermute(here, "core", [(k, nc - 1 - k) for k in range(nc)])
    slope, projected, damping = pl.pallas_call(
        begin,
        out_shape=(
            jax.ShapeDtypeStruct((center_rows, outputs), f32),
            jax.ShapeDtypeStruct((eigen, outputs), f32),
            jax.ShapeDtypeStruct((eigen, 1), f32),
        ),
        in_specs=[hbm, hbm, vmem],
        out_specs=(vmem, vmem, vmem),
        scratch_shapes=[
            VMEM(kernel_here.shape, bf16),
            VMEM((1, eigen), f32),
            pltpu.SemaphoreType.DMA((2,)),
        ],
        compiler_params=small,
    )(
        pltpu.with_memory_space_constraint(kernel_here, pltpu.HBM),
        pltpu.with_memory_space_constraint(damping.reshape(1, eigen), pltpu.HBM),
        here,
    )
    steps = 4
    updated = pl.pallas_call(
        functools.partial(update, steps),
        out_shape=jax.ShapeDtypeStruct((center_rows, outputs), bf16),
        in_specs=[vmem] * 7,
        out_specs=hbm,
        scratch_shapes=[
            VMEM((center_rows, outputs), bf16),
            pltpu.SemaphoreType.DMA((steps,)),
        ],
        compiler_params=small,
    )(kernel_there, there, slope, projected, local_basis, damping, weights)
    return (updated, residual)


def solution(mesh):
    devices = mesh.devices
    fine = Mesh(
        devices.reshape(4, devices.shape[0] // 8, 2, devices.shape[1]),
        ("x", "z", "core", "batch"),
    )
    center = ("x", "z", "core")
    return jax.shard_map(
        per_device,
        mesh=fine,
        in_specs=(
            P(center, None),
            P(center, None),
            P(center),
            P(center, None),
            P(),
            P("batch", center, None),
            P("batch", center, None),
            P("batch", center),
        ),
        out_specs=(P(center, None), P("batch", center, None)),
        check_vma=False,
    )
```

time: 130 us -> 120 us (0.923)
  matrix products: 9.47 us -> 0 us
  Pallas kernels: 0 us -> 8.23 us
  other arithmetic: 4.46 us -> 0.27 us
  starting transfers between devices: 13 us -> 10.8 us
  waiting for transfers between devices: 10.3 us -> 8.79 us
    dot_general x9 -> x0, matrix products: 9.47 us -> none  [the longest x4 6.46 us: rows_dot(): lax.dot_general(left, right, (((0,), (0,)), ((), ())), preferred_element_...]
    pallas_call x0 -> x5, Pallas kernels: none -> 8.23 us  [the longest x1 1.96 us: per_device(): pl.pallas_call(spread, out_shape=(square, square), in_specs=[smem, vmem,...]
    select_n x7 -> x1, other arithmetic: 3.11 us -> 0.02 us  [per_device(): jnp.where(core == 0, far, near)]
    all_to_all x1, starting transfers between devices: 6.75 us -> 4.53 us  [exchange(): return lax.all_to_all(values, axes, split_axis=0, concat_axis=0, tiled=True)]
    all_gather x2 -> x1, blocking collectives: 7.77 us -> 5.89 us  [per_device(): lax.all_gather(jnp.concatenate([features[:, k:k + 128] for k in range(0,...]
    all_to_all x1, waiting for transfers between devices: 10.3 us -> 8.79 us  [exchange(): return lax.all_to_all(values, axes, split_axis=0, concat_axis=0, tiled=True)]
  transfers between devices with their start and end apart: 2 -> 2, of which waited for: 1 -> 1; matrix products, arithmetic and copies ran while one was open for 2% -> 0% of each run, Pallas kernels for 0% -> 3%
where the time goes in v2:
time: 120 us
  blocking collectives  88.5 us (74%)
  starting transfers between devices  10.8 us (9%)
  waiting for transfers between devices  8.79 us (7%)
  Pallas kernels  8.23 us (7%)
  local copies, waits for them, and re-layouts  2.44 us (2%)
    all_to_all x5, blocking collectives, exchange(): return lax.all_to_all(values, axes, split_axis=0, concat_axis=0, tiled=True)  82.6 us
    all_to_all x1, waiting for transfers between devices, exchange(): return lax.all_to_all(values, axes, split_axis=0, concat_axis=0, tiled=True)  8.79 us
    ppermute x1, starting transfers between devices, per_device(): there = lax.ppermute(here, 'core', [(k, nc - 1 - k) for k in range(nc)])  6.28 us
    all_gather x1, blocking collectives, per_device(): lax.all_gather(jnp.concatenate([features[:, k:k + 128] for k in range(0,...  5.89 us
    all_to_all x1, starting transfers between devices, exchange(): return lax.all_to_all(values, axes, split_axis=0, concat_axis=0, tiled=True)  4.53 us
  transfers between devices with their start and end apart: 2, of which 1 were waited for; matrix products, arithmetic and copies ran while one was open for 0% of the time, Pallas kernels for 3%

profile of v2, /device:TPU:1, one launch (start us, length us, event | category | flops | bytes accessed | tf_op | source)
XLA Modules:
  0.0 119.9 jit_solution(9681430957557120499)
XLA Ops:
  0.6 1.5 %shard_map.95 = (bf16[32,1408]{1,0:T(8,128)(2,1)S(1)}, f32[8,512]{1,0:T(8,128)S(1)}) custom-call(s32[1,2]{1,0:T(1,128)} %refs_0_.1, s32[1,96]{1,0:T(1,128)} %bitcast.41, bf16[96,256]{1,0:T(8,128)(2,1)} %refs_2_.1, bf16[64,384]{1,0:T(8,128)(2,1)} %bitcast.39, bf16[64,512]{1,0:T(8,128)(2,1)} %bitcast.38), custom_call_target="tpu_custom_call" | custom-call | tf_op jit(solution)/shard_map/pallas_call | solution.py:237
  2.2 27.3 %all_to_all.30 = bf16[16,2,1408]{2,1,0:T(2,128)(2,1)S(1)} all-to-all(bf16[16,2,1408]{2,1,0:T(2,128)(2,1)S(1)} %reshape.50), channel_id=1, replica_groups=mesh['x'=4,'z'=16,'core'=2,'batch'=4] {'z'}, dimensions={0} | all-to-all | bytes 180224 | tf_op jit(solution)/shard_map/all_to_all | solution.py:19
  29.6 0.1 broadcast_in_dim.8
  29.7 16.9 %all_to_all.31 = bf16[16,32,640]{2,1,0:T(8,128)(2,1)S(1)} all-to-all(bf16[16,32,640]{2,1,0:T(8,128)(2,1)S(1)} %bitcast.33), channel_id=1, replica_groups=mesh['x'=4,'z'=16,'core'=2,'batch'=4] {'batch','x'}, dimensions={0} | all-to-all | bytes 1310720 | tf_op jit(solution)/shard_map/all_to_all | solution.py:19
  46.8 0.0 copy-start
  46.8 0.0 copy-start.1
  46.8 5.9 %all-gather = bf16[3968,128]{1,0:T(8,128)(2,1)S(1)} all-gather(bf16[1984,128]{1,0:T(8,128)(2,1)S(1)} %constant_dynamic-update-slice_fusion), channel_id=2, replica_groups=mesh['x'=4,'z'=16,'core'=2,'batch'=4] {'core'}, dimensions={0}, use_global_device_ids=true | all-gather | bytes 1523712 | tf_op jit(solution)/shard_map/all_gather | solution.py:290
  52.7 0.1 pad_add_fusion.place_ref
  52.8 1.7 %shard_map.96 = (bf16[256,768]{1,0:T(8,128)(2,1)S(1)}, bf16[512,256]{1,0:T(8,128)(2,1)S(1)}) custom-call(s32[2]{0:T(128)S(1)} %pad_add_fusion.place_ref, bf16[512,384]{1,0:T(8,128)(2,1)S(1)} %bitcast.28, bf16[448,128]{1,0:T(8,128)(2,1)S(1)} %pad_maximum_fusion.1.kept_ref, bf16[2,1984,128]{2,1,0:T(8,128)(2,1)S(1)} %bitcast.23, ...), custom_call_target="tpu_custom_call" | custom-call | tf_op jit(solution)/shard_map/pallas_call | solution.py:297
  54.5 10.8 %all_to_all.32 = bf16[8,32,768]{2,1,0:T(8,128)(2,1)S(1)} all-to-all(bf16[8,32,768]{2,1,0:T(8,128)(2,1)S(1)} %bitcast.32), channel_id=1, replica_groups=mesh['x'=4,'z'=16,'core'=2,'batch'=4] {'core','x'}, dimensions={0} | all-to-all | bytes 786432 | tf_op jit(solution)/shard_map/all_to_all | solution.py:19
  65.3 0.1 reduce_sum.21
  65.3 0.6 reshape.55
  66.0 4.5 %all-to-all-start.3 = ((bf16[16,2,768]{2,1,0:T(2,128)(2,1)}), bf16[16,2,768]{2,1,0:T(2,128)(2,1)S(1)}, u32[]{:S(2)}, u32[]{:S(2)}) async-start(bf16[16,2,768]{2,1,0:T(2,128)(2,1)} %reshape.55), calls=%async_computation.3 | async-start | bytes 98304 | tf_op jit(solution)/shard_map/all_to_all | solution.py:19
  70.5 2.0 %shard_map.97 = (bf16[512,512]{1,0:T(8,128)(2,1)S(1)}, bf16[512,512]{1,0:T(8,128)(2,1)S(1)}) custom-call(s32[2]{0:T(128)S(1)} %pad_add_fusion.place_ref, bf16[512,384]{1,0:T(8,128)(2,1)S(1)} %bitcast.29, bf16[2,1984,128]{2,1,0:T(8,128)(2,1)S(1)} %bitcast.24, bf16[512,384]{1,0:T(8,128)(2,1)S(1)} %copy-done.1), custom_call_target="tpu_custom_call" | custom-call | tf_op jit(solution)/shard_map/pallas_call | solution.py:312
  72.5 0.0 copy-start.2
  72.5 0.8 copy-done.2
  73.3 8.8 %all-to-all-done.3 = bf16[16,2,768]{2,1,0:T(2,128)(2,1)S(1)} async-done(((bf16[16,2,768]{2,1,0:T(2,128)(2,1)}), bf16[16,2,768]{2,1,0:T(2,128)(2,1)S(1)}, u32[]{:S(2)}, u32[]{:S(2)}) %all-to-all-start.3) | async-done | bytes 49184 | tf_op jit(solution)/shard_map/all_to_all | solution.py:19
  82.2 14.0 %all_to_all.33 = bf16[16,2,768]{2,1,0:T(2,128)(2,1)S(1)} all-to-all(bf16[16,2,768]{2,1,0:T(2,128)(2,1)S(1)} %broadcast_in_dim.9), channel_id=1, replica_groups=mesh['x'=4,'z'=16,'core'=2,'batch'=4] {'z'}, dimensions={0} | all-to-all | bytes 98304 | tf_op jit(solution)/shard_map/all_to_all | solution.py:19
  96.2 0.1 broadcast_in_dim.22
  96.3 13.6 %all_to_all.34 = bf16[16,32,768]{2,1,0:T(8,128)(2,1)S(1)} all-to-all(bf16[16,32,768]{2,1,0:T(8,128)(2,1)S(1)} %broadcast_in_dim.22), channel_id=1, replica_groups=mesh['x'=4,'z'=16,'core'=2,'batch'=4] {'batch','x'}, dimensions={0} | all-to-all | bytes 1572864 | tf_op jit(solution)/shard_map/all_to_all | solution.py:19
  110.0 6.3 %collective-permute-start = (bf16[512,768]{1,0:T(8,128)(2,1)S(1)}, bf16[512,768]{1,0:T(8,128)(2,1)S(1)}, u32[]{:S(2)}, u32[]{:S(2)}) collective-permute-start(bf16[512,768]{1,0:T(8,128)(2,1)S(1)} %bitcast.30), channel_id=1, source_target_pairs={{0,4},{4,0},{1,5},{5,1},{2,6},{6,2},{3,7},{7,3},{8,12},{12,8},{9,1... | collective-permute-start | bytes 2359304 | tf_op jit(solution)/shard_map/ppermute | solution.py:333
  116.3 1.5 %shard_map.98 = (f32[512,512]{1,0:T(8,128)S(1)}, f32[256,512]{1,0:T(8,128)S(1)}, f32[256,1]{1,0:T(8,128)S(1)}) custom-call(bf16[512,512]{1,0:T(8,128)(2,1)} %copy-done.2, f32[1,256]{1,0:T(1,128)} %bitcast.40, bf16[512,768]{1,0:T(8,128)(2,1)S(1)} %bitcast.31), custom_call_target="tpu_custom_call" | custom-call | tf_op jit(solution)/shard_map/pallas_call | solution.py:334
  117.8 0.6 constant_dynamic-slice_fusion
  118.4 1.6 %shard_map.99 = bf16[512,512]{1,0:T(8,128)(2,1)} custom-call(bf16[512,512]{1,0:T(8,128)(2,1)S(1)} %get-tuple-element.41.kernel_ref, bf16[512,768]{1,0:T(8,128)(2,1)S(1)} %collective-permute-done.there_ref, f32[512,512]{1,0:T(8,128)S(1)} %get-tuple-element.44.slope_ref, f32[256,512]{1,0:T(8,128)S(1)} %get-tuple-element.45.project_ref, ...), custom_call_target="tpu_custom_call" | custom-call | tf_op jit(solution)/shard_map/pallas_call | solution.py:355
  (27 shorter events, 0.4 us)
Async XLA Ops:
  46.8 6.0 %copy-start = (bf16[512,512]{1,0:T(8,128)(2,1)S(1)}, bf16[512,512]{1,0:T(8,128)(2,1)}, u32[]{:S(2)}) copy-start(bf16[512,512]{1,0:T(8,128)(2,1)} %weights_ref.3) | copy-start | bytes 1572868
  46.8 6.0 %copy-start.1 = (bf16[512,384]{1,0:T(8,128)(2,1)S(1)}, bf16[512,384]{1,0:T(8,128)(2,1)}, u32[]{:S(2)}) copy-start(bf16[512,384]{1,0:T(8,128)(2,1)} %centers_ref.3) | copy-start | bytes 1179652
  66.0 16.1 %all-to-all-start.3 = ((bf16[16,2,768]{2,1,0:T(2,128)(2,1)}), bf16[16,2,768]{2,1,0:T(2,128)(2,1)S(1)}, u32[]{:S(2)}, u32[]{:S(2)}) async-start(bf16[16,2,768]{2,1,0:T(2,128)(2,1)} %reshape.55), calls=%async_computation.3 | async-start | bytes 98304 | tf_op jit(solution)/shard_map/all_to_all | solution.py:19
  72.5 0.8 copy-start.2
  110.0 8.4 %collective-permute-start = (bf16[512,768]{1,0:T(8,128)(2,1)S(1)}, bf16[512,768]{1,0:T(8,128)(2,1)S(1)}, u32[]{:S(2)}, u32[]{:S(2)}) collective-permute-start(bf16[512,768]{1,0:T(8,128)(2,1)S(1)} %bitcast.30), channel_id=1, source_target_pairs={{0,4},{4,0},{1,5},{5,1},{2,6},{6,2},{3,7},{7,3},{8,12},{12,8},{9,1... | collective-permute-start | bytes 2359304 | tf_op jit(solution)/shard_map/ppermute | solution.py:333

commit v3 on v2

--- a/solution.py
+++ b/solution.py
@@ -15,8 +15,25 @@
 VMEM = pltpu.VMEM
 
 
-def exchange(values, axes):
-    return lax.all_to_all(values, axes, split_axis=0, concat_axis=0, tiled=True)
+def far_first(size):
+    return [(k + size // 2) % size for k in range(size)]
+
+
+def exchange(values, *axes):
+    order = [0]
+    for axis in axes:
+        size = lax.axis_size(axis)
+        own = range(size) if axis == "core" else far_first(size)
+        order = [k * size + j for k in order for j in own]
+    names = axes if len(axes) > 1 else axes[0]
+    return lax.all_to_all(
+        values, names, split_axis=0, concat_axis=0, tiled=True, axis_index_groups=[order]
+    )
+
+
+def spot(axis):
+    size = lax.axis_size(axis)
+    return lax.rem(lax.axis_index(axis) + size // 2, size)
 
 
 def iota(shape, dim):
@@ -48,8 +65,8 @@
     for copy in copies:
         copy.wait()
     entries, eigen = basis_ref.shape
-    group = lax.axis_index("batch")
-    upper = jnp.where(lax.axis_index("x") < nx // 2, 0, eigen // 8)
+    group = spot("batch")
+    upper = jnp.where(spot("x") < nx // 2, 0, eigen // 8)
     half = eigen // 2
     depth, width = stored_ref.shape
     index = index_ref[...]
@@ -72,11 +89,12 @@
     carried = jnp.where(group < capacity, kept, position)
     carried = jnp.concatenate([carried[:, :half], carried[:, half:]], axis=0)
     line_bits = (nz * nc).bit_length() - 1
-    corner = lax.shift_right_logical(column_holder, line_bits) * nc + lax.bitwise_and(
-        column_holder, nc - 1
-    )
+    across = lax.shift_right_logical(column_holder, line_bits)
+    across = lax.bitwise_and(across + nx // 2, nx - 1)
+    corner = across * nc + lax.bitwise_and(column_holder, nc - 1)
     corner = jnp.concatenate([corner, corner], axis=0)
     line = lax.shift_right_logical(lax.bitwise_and(holder, nz * nc - 1), nc.bit_length() - 1)
+    line = lax.bitwise_and(line + nz // 2, nz - 1)
     here = iota((2 * nz, entries), 0)
     same = lax.shift_right_logical(here, 1) == line
     odd = lax.bitwise_and(here, 1)
@@ -227,7 +245,7 @@
     side = nx * block
     wide = outputs + eigen
     half = eigen // 2
-    group = lax.axis_index("batch")
+    group = spot("batch")
     core = lax.axis_index("core")
     smem = pl.BlockSpec(memory_space=pltpu.SMEM)
     vmem = pl.BlockSpec(memory_space=VMEM)
@@ -276,7 +294,7 @@
     )
     second = jnp.broadcast_to(second[None], (ny, nx, block, width + eigen))
     second, group, core = lax.optimization_barrier((second, group, core))
-    second = exchange(second.reshape(ny * nx, block, width + eigen), ("batch", "x"))
+    second = exchange(second.reshape(ny * nx, block, width + eigen), "batch", "x")
     second, group, core = lax.optimization_barrier((second, group, core))
     features = second[:, :, :width].reshape(ny * side, width)
     near = second[:, :, width : width + half].reshape(ny * side, half)
@@ -304,7 +322,7 @@
         out_specs=(vmem, vmem),
         compiler_params=small,
     )(place, features, kept, pair, centers, weights)
-    partial = exchange(partial.reshape(nc * nx, block, wide), ("core", "x"))
+    partial = exchange(partial.reshape(nc * nx, block, wide), "core", "x")
     partial = jnp.sum(partial.astype(f32), axis=0).astype(bf16)
     partial, place = lax.optimization_barrier((partial, place))
     partial = exchange(partial.reshape(nz, own_rows, wide), "z")
@@ -323,10 +341,10 @@
 
     own_all = exchange(jnp.broadcast_to(own[None], (nz, own_rows, wide)), "z")
     own_all = jnp.broadcast_to(own_all.reshape(1, block, wide), (ny * nx, block, wide))
-    here = exchange(own_all, ("batch", "x"))
+    here = exchange(own_all, "batch", "x")
     residual = lax.dynamic_slice(
         here,
-        (group * nx + lax.axis_index("x"), lax.axis_index("z") * own_rows, 0),
+        (spot("batch") * nx + spot("x"), spot("z") * own_rows, 0),
         (1, own_rows, outputs),
     )
     here = here.reshape(ny * side, wide)

time: 120 us -> 112 us (0.933)
  waiting for transfers between devices: 8.79 us -> 0.02 us
  starting transfers between devices: 10.8 us -> 15.4 us
  blocking collectives: 88.5 us -> 84.3 us
    all_to_all x1, waiting for transfers between devices: 8.79 us -> 0.02 us  [exchange(): lax.all_to_all(values, names, split_axis=0, concat_axis=0, tiled=True, ax...]
    all_to_all x1, starting transfers between devices: 4.53 us -> 11.5 us  [exchange(): lax.all_to_all(values, names, split_axis=0, concat_axis=0, tiled=True, ax...]
    all_gather x1, blocking collectives: 5.89 us -> 2.79 us  [per_device(): lax.all_gather(jnp.concatenate([features[:, k:k + 128] for k in range(0,...]
    ppermute x1, starting transfers between devices: 6.28 us -> 3.88 us  [per_device(): there = lax.ppermute(here, 'core', [(k, nc - 1 - k) for k in range(nc)])]
  transfers between devices with their start and end apart: 2 -> 2, of which waited for: 1 -> 0; matrix products, arithmetic and copies ran while one was open for 0% -> 1% of each run, Pallas kernels for 3% -> 3%
where the time goes in v3:
time: 112 us; the launch traced here: 111 us
  blocking collectives  84.3 us (75%)
  starting transfers between devices  15.4 us (14%)
  Pallas kernels  8.23 us (7%)
  local copies, waits for them, and re-layouts  2.44 us (2%)
    all_to_all x5, blocking collectives, exchange(): lax.all_to_all(values, names, split_axis=0, concat_axis=0, tiled=True, ax...  81.5 us
    all_to_all x1, starting transfers between devices, exchange(): lax.all_to_all(values, names, split_axis=0, concat_axis=0, tiled=True, ax...  11.5 us
    ppermute x1, starting transfers between devices, per_device(): there = lax.ppermute(here, 'core', [(k, nc - 1 - k) for k in range(nc)])  3.88 us
    all_gather x1, blocking collectives, per_device(): lax.all_gather(jnp.concatenate([features[:, k:k + 128] for k in range(0,...  2.79 us
  transfers between devices with their start and end apart: 2, of which 0 were waited for; matrix products, arithmetic and copies ran while one was open for 1% of the time, Pallas kernels for 3%

profile of v3, /device:TPU:1, one launch (start us, length us, event | category | flops | bytes accessed | tf_op | source)
XLA Modules:
  0.0 111.5 jit_solution(15182703636983197264)
XLA Ops:
  0.6 1.5 %shard_map.95 = (bf16[32,1408]{1,0:T(8,128)(2,1)S(1)}, f32[8,512]{1,0:T(8,128)S(1)}) custom-call(s32[1,2]{1,0:T(1,128)} %refs_0_.1, s32[1,96]{1,0:T(1,128)} %bitcast.41, bf16[96,256]{1,0:T(8,128)(2,1)} %refs_2_.1, bf16[64,384]{1,0:T(8,128)(2,1)} %bitcast.39, bf16[64,512]{1,0:T(8,128)(2,1)} %bitcast.38), custom_call_target="tpu_custom_call" | custom-call | tf_op jit(solution)/shard_map/pallas_call | solution.py:255
  2.2 23.8 %all_to_all.30 = bf16[16,2,1408]{2,1,0:T(2,128)(2,1)S(1)} all-to-all(bf16[16,2,1408]{2,1,0:T(2,128)(2,1)S(1)} %reshape.50), channel_id=1, replica_groups={{64,72,80,88,96,104,112,120,0,8,16,24,32,40,48,56},{65,73,81,89,97,105,..., dimensions={0} | all-to-all | bytes 180224 | tf_op jit(solution)/shard_map/all_to_all | solution.py:29
  26.1 0.1 broadcast_in_dim.8
  26.1 16.7 %all_to_all.31 = bf16[16,32,640]{2,1,0:T(8,128)(2,1)S(1)} all-to-all(bf16[16,32,640]{2,1,0:T(8,128)(2,1)S(1)} %bitcast.33), channel_id=1, replica_groups={{258,386,2,130,259,387,3,131,256,384,0,128,257,385,1,129},{262,390,6,13..., dimensions={0} | all-to-all | bytes 1310720 | tf_op jit(solution)/shard_map/all_to_all | solution.py:29
  43.1 0.0 copy-start
  43.1 0.0 copy-start.1
  43.1 2.8 %all-gather = bf16[3968,128]{1,0:T(8,128)(2,1)S(1)} all-gather(bf16[1984,128]{1,0:T(8,128)(2,1)S(1)} %constant_dynamic-update-slice_fusion), channel_id=2, replica_groups=mesh['x'=4,'z'=16,'core'=2,'batch'=4] {'core'}, dimensions={0}, use_global_device_ids=true | all-gather | bytes 1523712 | tf_op jit(solution)/shard_map/all_gather | solution.py:308
  45.9 0.1 pad_add_fusion.place_ref
  46.0 1.7 %shard_map.96 = (bf16[256,768]{1,0:T(8,128)(2,1)S(1)}, bf16[512,256]{1,0:T(8,128)(2,1)S(1)}) custom-call(s32[2]{0:T(128)S(1)} %pad_add_fusion.place_ref, bf16[512,384]{1,0:T(8,128)(2,1)S(1)} %bitcast.28, bf16[448,128]{1,0:T(8,128)(2,1)S(1)} %pad_maximum_fusion.1.kept_ref, bf16[2,1984,128]{2,1,0:T(8,128)(2,1)S(1)} %bitcast.23, ...), custom_call_target="tpu_custom_call" | custom-call | tf_op jit(solution)/shard_map/pallas_call | solution.py:315
  47.8 11.1 %all_to_all.32 = bf16[8,32,768]{2,1,0:T(8,128)(2,1)S(1)} all-to-all(bf16[8,32,768]{2,1,0:T(8,128)(2,1)S(1)} %bitcast.32), channel_id=1, replica_groups={{256,384,0,128,260,388,4,132},{257,385,1,129,261,389,5,133},{258,386,2,..., dimensions={0} | all-to-all | bytes 786432 | tf_op jit(solution)/shard_map/all_to_all | solution.py:29
  58.9 0.1 reduce_sum.21
  58.9 0.6 reshape.55
  59.6 11.5 %all-to-all-start.3 = ((bf16[16,2,768]{2,1,0:T(2,128)(2,1)}), bf16[16,2,768]{2,1,0:T(2,128)(2,1)S(1)}, u32[]{:S(2)}, u32[]{:S(2)}) async-start(bf16[16,2,768]{2,1,0:T(2,128)(2,1)} %reshape.55), calls=%async_computation.3 | async-start | bytes 98304 | tf_op jit(solution)/shard_map/all_to_all | solution.py:29
  71.0 2.0 %shard_map.97 = (bf16[512,512]{1,0:T(8,128)(2,1)S(1)}, bf16[512,512]{1,0:T(8,128)(2,1)S(1)}) custom-call(s32[2]{0:T(128)S(1)} %pad_add_fusion.place_ref, bf16[512,384]{1,0:T(8,128)(2,1)S(1)} %bitcast.29, bf16[2,1984,128]{2,1,0:T(8,128)(2,1)S(1)} %bitcast.24, bf16[512,384]{1,0:T(8,128)(2,1)S(1)} %copy-done.1), custom_call_target="tpu_custom_call" | custom-call | tf_op jit(solution)/shard_map/pallas_call | solution.py:330
  73.0 0.0 copy-start.2
  73.0 0.8 copy-done.2
  73.8 0.0 all-to-all-done.3
  73.9 14.1 %all_to_all.33 = bf16[16,2,768]{2,1,0:T(2,128)(2,1)S(1)} all-to-all(bf16[16,2,768]{2,1,0:T(2,128)(2,1)S(1)} %broadcast_in_dim.9), channel_id=1, replica_groups={{64,72,80,88,96,104,112,120,0,8,16,24,32,40,48,56},{65,73,81,89,97,105,..., dimensions={0} | all-to-all | bytes 98304 | tf_op jit(solution)/shard_map/all_to_all | solution.py:29
  88.0 0.1 broadcast_in_dim.22
  88.1 15.8 %all_to_all.34 = bf16[16,32,768]{2,1,0:T(8,128)(2,1)S(1)} all-to-all(bf16[16,32,768]{2,1,0:T(8,128)(2,1)S(1)} %broadcast_in_dim.22), channel_id=1, replica_groups={{258,386,2,130,259,387,3,131,256,384,0,128,257,385,1,129},{262,390,6,13..., dimensions={0} | all-to-all | bytes 1572864 | tf_op jit(solution)/shard_map/all_to_all | solution.py:29
  103.9 3.9 %collective-permute-start = (bf16[512,768]{1,0:T(8,128)(2,1)S(1)}, bf16[512,768]{1,0:T(8,128)(2,1)S(1)}, u32[]{:S(2)}, u32[]{:S(2)}) collective-permute-start(bf16[512,768]{1,0:T(8,128)(2,1)S(1)} %bitcast.30), channel_id=1, source_target_pairs={{0,4},{4,0},{1,5},{5,1},{2,6},{6,2},{3,7},{7,3},{8,12},{12,8},{9,1... | collective-permute-start | bytes 2359304 | tf_op jit(solution)/shard_map/ppermute | solution.py:351
  107.8 1.5 %shard_map.98 = (f32[512,512]{1,0:T(8,128)S(1)}, f32[256,512]{1,0:T(8,128)S(1)}, f32[256,1]{1,0:T(8,128)S(1)}) custom-call(bf16[512,512]{1,0:T(8,128)(2,1)} %copy-done.2, f32[1,256]{1,0:T(1,128)} %bitcast.40, bf16[512,768]{1,0:T(8,128)(2,1)S(1)} %bitcast.31), custom_call_target="tpu_custom_call" | custom-call | tf_op jit(solution)/shard_map/pallas_call | solution.py:352
  109.3 0.6 constant_dynamic-slice_fusion
  109.9 1.6 %shard_map.99 = bf16[512,512]{1,0:T(8,128)(2,1)} custom-call(bf16[512,512]{1,0:T(8,128)(2,1)S(1)} %get-tuple-element.41.kernel_ref, bf16[512,768]{1,0:T(8,128)(2,1)S(1)} %collective-permute-done.there_ref, f32[512,512]{1,0:T(8,128)S(1)} %get-tuple-element.44.slope_ref, f32[256,512]{1,0:T(8,128)S(1)} %get-tuple-element.45.project_ref, ...), custom_call_target="tpu_custom_call" | custom-call | tf_op jit(solution)/shard_map/pallas_call | solution.py:373
  (27 shorter events, 0.4 us)
Async XLA Ops:
  43.1 2.9 %copy-start = (bf16[512,512]{1,0:T(8,128)(2,1)S(1)}, bf16[512,512]{1,0:T(8,128)(2,1)}, u32[]{:S(2)}) copy-start(bf16[512,512]{1,0:T(8,128)(2,1)} %weights_ref.3) | copy-start | bytes 1572868
  43.1 2.9 %copy-start.1 = (bf16[512,384]{1,0:T(8,128)(2,1)S(1)}, bf16[512,384]{1,0:T(8,128)(2,1)}, u32[]{:S(2)}) copy-start(bf16[512,384]{1,0:T(8,128)(2,1)} %centers_ref.3) | copy-start | bytes 1179652
  59.6 14.3 %all-to-all-start.3 = ((bf16[16,2,768]{2,1,0:T(2,128)(2,1)}), bf16[16,2,768]{2,1,0:T(2,128)(2,1)S(1)}, u32[]{:S(2)}, u32[]{:S(2)}) async-start(bf16[16,2,768]{2,1,0:T(2,128)(2,1)} %reshape.55), calls=%async_computation.3 | async-start | bytes 98304 | tf_op jit(solution)/shard_map/all_to_all | solution.py:29
  73.0 0.8 copy-start.2
  103.9 6.0 %collective-permute-start = (bf16[512,768]{1,0:T(8,128)(2,1)S(1)}, bf16[512,768]{1,0:T(8,128)(2,1)S(1)}, u32[]{:S(2)}, u32[]{:S(2)}) collective-permute-start(bf16[512,768]{1,0:T(8,128)(2,1)S(1)} %bitcast.30), channel_id=1, source_target_pairs={{0,4},{4,0},{1,5},{5,1},{2,6},{6,2},{3,7},{7,3},{8,12},{12,8},{9,1... | collective-permute-start | bytes 2359304 | tf_op jit(solution)/shard_map/ppermute | solution.py:351

commit v4 on v3

--- a/solution.py
+++ b/solution.py
@@ -138,16 +138,14 @@
         return laplace(squares(features) + line - 2.0 * cross)
 
     start = pl.multiple_of(group * side, side)
-    near = across(features_ref[pl.ds(start, side), :])
-    far = across(
-        jnp.concatenate(
-            [
-                pair_ref[other, pl.ds(pl.multiple_of(k * count + start, side), side), :]
-                for k in range(parts)
-            ],
-            axis=1,
-        )
-    )
+    far = jnp.concatenate(
+        [
+            pair_ref[other, pl.ds(pl.multiple_of(k * count + start, side), side), :]
+            for k in range(parts)
+        ],
+        axis=1,
+    )
+    kernel = across(jnp.concatenate([features_ref[pl.ds(start, side), :], far], axis=0))
 
     at = iota((rows, side), 0)
     parity = lax.bitwise_and(iota((1, side), 1), 1)
@@ -177,10 +175,13 @@
                 halves[h] = halves[h] + mxu(member, blocks[k])
     local = jnp.concatenate(halves, axis=1).astype(bf16)
     basis_ref[...] = local
-    for kernel, to in ((near, core), (far, other)):
-        spot = pl.ds(pl.multiple_of(to * side, side), side)
-        out_ref[spot, :outputs] = mxu(kernel, weights_ref[...]).astype(bf16)
-        out_ref[spot, outputs:] = mxu(kernel, local).astype(bf16)
+    for values, first in ((weights_ref[...], 0), (local, outputs)):
+        product = mxu(kernel, values).astype(bf16)
+        for k, to in ((0, core), (1, other)):
+            spot_rows = pl.ds(pl.multiple_of(to * side, side), side)
+            out_ref[spot_rows, first : first + values.shape[1]] = product[
+                k * side : (k + 1) * side, :
+            ]
 
 
 def spread(place_ref, features_ref, pair_ref, centers_ref, here_ref, there_ref):
@@ -369,7 +370,7 @@
         pltpu.with_memory_space_constraint(damping.reshape(1, eigen), pltpu.HBM),
         here,
     )
-    steps = 4
+    steps = 2
     updated = pl.pallas_call(
         functools.partial(update, steps),
         out_shape=jax.ShapeDtypeStruct((center_rows, outputs), bf16),

time: 112 us -> 112 us (level)
  no operation moved by 1% of the time
where the time goes in v4:
time: 112 us; the launch traced here: 111 us
  blocking collectives  84.3 us (75%)
  starting transfers between devices  15.4 us (14%)
  Pallas kernels  8.16 us (7%)
  local copies, waits for them, and re-layouts  2.44 us (2%)
    all_to_all x5, blocking collectives, exchange(): lax.all_to_all(values, names, split_axis=0, concat_axis=0, tiled=True, ax...  81.5 us
    all_to_all x1, starting transfers between devices, exchange(): lax.all_to_all(values, names, split_axis=0, concat_axis=0, tiled=True, ax...  11.5 us
    ppermute x1, starting transfers between devices, per_device(): there = lax.ppermute(here, 'core', [(k, nc - 1 - k) for k in range(nc)])  3.88 us
    all_gather x1, blocking collectives, per_device(): lax.all_gather(jnp.concatenate([features[:, k:k + 128] for k in range(0,...  2.79 us
  transfers between devices with their start and end apart: 2, of which 0 were waited for; matrix products, arithmetic and copies ran while one was open for 1% of the time, Pallas kernels for 3%

profile of v4, /device:TPU:1, one launch (start us, length us, event | category | flops | bytes accessed | tf_op | source)
XLA Modules:
  0.0 111.4 jit_solution(17054218233445573043)
XLA Ops:
  0.6 1.5 %shard_map.95 = (bf16[32,1408]{1,0:T(8,128)(2,1)S(1)}, f32[8,512]{1,0:T(8,128)S(1)}) custom-call(s32[1,2]{1,0:T(1,128)} %refs_0_.1, s32[1,96]{1,0:T(1,128)} %bitcast.41, bf16[96,256]{1,0:T(8,128)(2,1)} %refs_2_.1, bf16[64,384]{1,0:T(8,128)(2,1)} %bitcast.39, bf16[64,512]{1,0:T(8,128)(2,1)} %bitcast.38), custom_call_target="tpu_custom_call" | custom-call | tf_op jit(solution)/shard_map/pallas_call | solution.py:256
  2.2 23.8 %all_to_all.30 = bf16[16,2,1408]{2,1,0:T(2,128)(2,1)S(1)} all-to-all(bf16[16,2,1408]{2,1,0:T(2,128)(2,1)S(1)} %reshape.50), channel_id=1, replica_groups={{64,72,80,88,96,104,112,120,0,8,16,24,32,40,48,56},{65,73,81,89,97,105,..., dimensions={0} | all-to-all | bytes 180224 | tf_op jit(solution)/shard_map/all_to_all | solution.py:29
  26.1 0.1 broadcast_in_dim.8
  26.1 16.7 %all_to_all.31 = bf16[16,32,640]{2,1,0:T(8,128)(2,1)S(1)} all-to-all(bf16[16,32,640]{2,1,0:T(8,128)(2,1)S(1)} %bitcast.33), channel_id=1, replica_groups={{258,386,2,130,259,387,3,131,256,384,0,128,257,385,1,129},{262,390,6,13..., dimensions={0} | all-to-all | bytes 1310720 | tf_op jit(solution)/shard_map/all_to_all | solution.py:29
  43.1 0.0 copy-start
  43.1 0.0 copy-start.1
  43.1 2.8 %all-gather = bf16[3968,128]{1,0:T(8,128)(2,1)S(1)} all-gather(bf16[1984,128]{1,0:T(8,128)(2,1)S(1)} %constant_dynamic-update-slice_fusion), channel_id=2, replica_groups=mesh['x'=4,'z'=16,'core'=2,'batch'=4] {'core'}, dimensions={0}, use_global_device_ids=true | all-gather | bytes 1523712 | tf_op jit(solution)/shard_map/all_gather | solution.py:309
  45.9 0.1 pad_add_fusion.place_ref
  46.0 1.7 %shard_map.96 = (bf16[256,768]{1,0:T(8,128)(2,1)S(1)}, bf16[512,256]{1,0:T(8,128)(2,1)S(1)}) custom-call(s32[2]{0:T(128)S(1)} %pad_add_fusion.place_ref, bf16[512,384]{1,0:T(8,128)(2,1)S(1)} %bitcast.28, bf16[448,128]{1,0:T(8,128)(2,1)S(1)} %pad_maximum_fusion.1.kept_ref, bf16[2,1984,128]{2,1,0:T(8,128)(2,1)S(1)} %bitcast.23, ...), custom_call_target="tpu_custom_call" | custom-call | tf_op jit(solution)/shard_map/pallas_call | solution.py:316
  47.7 11.1 %all_to_all.32 = bf16[8,32,768]{2,1,0:T(8,128)(2,1)S(1)} all-to-all(bf16[8,32,768]{2,1,0:T(8,128)(2,1)S(1)} %bitcast.32), channel_id=1, replica_groups={{256,384,0,128,260,388,4,132},{257,385,1,129,261,389,5,133},{258,386,2,..., dimensions={0} | all-to-all | bytes 786432 | tf_op jit(solution)/shard_map/all_to_all | solution.py:29
  58.8 0.1 reduce_sum.21
  58.9 0.6 reshape.55
  59.5 11.5 %all-to-all-start.3 = ((bf16[16,2,768]{2,1,0:T(2,128)(2,1)}), bf16[16,2,768]{2,1,0:T(2,128)(2,1)S(1)}, u32[]{:S(2)}, u32[]{:S(2)}) async-start(bf16[16,2,768]{2,1,0:T(2,128)(2,1)} %reshape.55), calls=%async_computation.3 | async-start | bytes 98304 | tf_op jit(solution)/shard_map/all_to_all | solution.py:29
  71.0 2.0 %shard_map.97 = (bf16[512,512]{1,0:T(8,128)(2,1)S(1)}, bf16[512,512]{1,0:T(8,128)(2,1)S(1)}) custom-call(s32[2]{0:T(128)S(1)} %pad_add_fusion.place_ref, bf16[512,384]{1,0:T(8,128)(2,1)S(1)} %bitcast.29, bf16[2,1984,128]{2,1,0:T(8,128)(2,1)S(1)} %bitcast.24, bf16[512,384]{1,0:T(8,128)(2,1)S(1)} %copy-done.1), custom_call_target="tpu_custom_call" | custom-call | tf_op jit(solution)/shard_map/pallas_call | solution.py:331
  72.9 0.0 copy-start.2
  73.0 0.8 copy-done.2
  73.7 0.0 all-to-all-done.3
  73.9 14.1 %all_to_all.33 = bf16[16,2,768]{2,1,0:T(2,128)(2,1)S(1)} all-to-all(bf16[16,2,768]{2,1,0:T(2,128)(2,1)S(1)} %broadcast_in_dim.9), channel_id=1, replica_groups={{64,72,80,88,96,104,112,120,0,8,16,24,32,40,48,56},{65,73,81,89,97,105,..., dimensions={0} | all-to-all | bytes 98304 | tf_op jit(solution)/shard_map/all_to_all | solution.py:29
  88.0 0.1 broadcast_in_dim.22
  88.1 15.8 %all_to_all.34 = bf16[16,32,768]{2,1,0:T(8,128)(2,1)S(1)} all-to-all(bf16[16,32,768]{2,1,0:T(8,128)(2,1)S(1)} %broadcast_in_dim.22), channel_id=1, replica_groups={{258,386,2,130,259,387,3,131,256,384,0,128,257,385,1,129},{262,390,6,13..., dimensions={0} | all-to-all | bytes 1572864 | tf_op jit(solution)/shard_map/all_to_all | solution.py:29
  103.8 3.9 %collective-permute-start = (bf16[512,768]{1,0:T(8,128)(2,1)S(1)}, bf16[512,768]{1,0:T(8,128)(2,1)S(1)}, u32[]{:S(2)}, u32[]{:S(2)}) collective-permute-start(bf16[512,768]{1,0:T(8,128)(2,1)S(1)} %bitcast.30), channel_id=1, source_target_pairs={{0,4},{4,0},{1,5},{5,1},{2,6},{6,2},{3,7},{7,3},{8,12},{12,8},{9,1... | collective-permute-start | bytes 2359304 | tf_op jit(solution)/shard_map/ppermute | solution.py:352
  107.8 1.5 %shard_map.98 = (f32[512,512]{1,0:T(8,128)S(1)}, f32[256,512]{1,0:T(8,128)S(1)}, f32[256,1]{1,0:T(8,128)S(1)}) custom-call(bf16[512,512]{1,0:T(8,128)(2,1)} %copy-done.2, f32[1,256]{1,0:T(1,128)} %bitcast.40, bf16[512,768]{1,0:T(8,128)(2,1)S(1)} %bitcast.31), custom_call_target="tpu_custom_call" | custom-call | tf_op jit(solution)/shard_map/pallas_call | solution.py:353
  109.3 0.6 constant_dynamic-slice_fusion
  109.9 1.5 %shard_map.99 = bf16[512,512]{1,0:T(8,128)(2,1)} custom-call(bf16[512,512]{1,0:T(8,128)(2,1)S(1)} %get-tuple-element.41.kernel_ref, bf16[512,768]{1,0:T(8,128)(2,1)S(1)} %collective-permute-done.there_ref, f32[512,512]{1,0:T(8,128)S(1)} %get-tuple-element.44.slope_ref, f32[256,512]{1,0:T(8,128)S(1)} %get-tuple-element.45.project_ref, ...), custom_call_target="tpu_custom_call" | custom-call | tf_op jit(solution)/shard_map/pallas_call | solution.py:374
  (27 shorter events, 0.4 us)
Async XLA Ops:
  43.1 2.9 %copy-start = (bf16[512,512]{1,0:T(8,128)(2,1)S(1)}, bf16[512,512]{1,0:T(8,128)(2,1)}, u32[]{:S(2)}) copy-start(bf16[512,512]{1,0:T(8,128)(2,1)} %weights_ref.3) | copy-start | bytes 1572868
  43.1 2.9 %copy-start.1 = (bf16[512,384]{1,0:T(8,128)(2,1)S(1)}, bf16[512,384]{1,0:T(8,128)(2,1)}, u32[]{:S(2)}) copy-start(bf16[512,384]{1,0:T(8,128)(2,1)} %centers_ref.3) | copy-start | bytes 1179652
  59.5 14.3 %all-to-all-start.3 = ((bf16[16,2,768]{2,1,0:T(2,128)(2,1)}), bf16[16,2,768]{2,1,0:T(2,128)(2,1)S(1)}, u32[]{:S(2)}, u32[]{:S(2)}) async-start(bf16[16,2,768]{2,1,0:T(2,128)(2,1)} %reshape.55), calls=%async_computation.3 | async-start | bytes 98304 | tf_op jit(solution)/shard_map/all_to_all | solution.py:29
  72.9 0.8 copy-start.2
  103.8 6.0 %collective-permute-start = (bf16[512,768]{1,0:T(8,128)(2,1)S(1)}, bf16[512,768]{1,0:T(8,128)(2,1)S(1)}, u32[]{:S(2)}, u32[]{:S(2)}) collective-permute-start(bf16[512,768]{1,0:T(8,128)(2,1)S(1)} %bitcast.30), channel_id=1, source_target_pairs={{0,4},{4,0},{1,5},{5,1},{2,6},{6,2},{3,7},{7,3},{8,12},{12,8},{9,1... | collective-permute-start | bytes 2359304 | tf_op jit(solution)/shard_map/ppermute | solution.py:352

commit v5 on v4

--- a/solution.py
+++ b/solution.py
@@ -15,15 +15,19 @@
 VMEM = pltpu.VMEM
 
 
-def far_first(size):
-    return [(k + size // 2) % size for k in range(size)]
+def origin(axis, size):
+    return 5 * size // 8 if axis == "z" else size // 2
+
+
+def far_first(axis, size):
+    return [(k + origin(axis, size)) % size for k in range(size)]
 
 
 def exchange(values, *axes):
     order = [0]
     for axis in axes:
         size = lax.axis_size(axis)
-        own = range(size) if axis == "core" else far_first(size)
+        own = range(size) if axis == "core" else far_first(axis, size)
         order = [k * size + j for k in order for j in own]
     names = axes if len(axes) > 1 else axes[0]
     return lax.all_to_all(
@@ -33,7 +37,7 @@
 
 def spot(axis):
     size = lax.axis_size(axis)
-    return lax.rem(lax.axis_index(axis) + size // 2, size)
+    return lax.rem(lax.axis_index(axis) + size - origin(axis, size), size)
 
 
 def iota(shape, dim):
@@ -94,7 +98,7 @@
     corner = across * nc + lax.bitwise_and(column_holder, nc - 1)
     corner = jnp.concatenate([corner, corner], axis=0)
     line = lax.shift_right_logical(lax.bitwise_and(holder, nz * nc - 1), nc.bit_length() - 1)
-    line = lax.bitwise_and(line + nz // 2, nz - 1)
+    line = lax.bitwise_and(line + nz - origin("z", nz), nz - 1)
     here = iota((2 * nz, entries), 0)
     same = lax.shift_right_logical(here, 1) == line
     odd = lax.bitwise_and(here, 1)

time: 112 us -> 112 us (level)
  waiting for transfers between devices: 0.02 us -> 1.72 us
  starting transfers between devices: 15.4 us -> 14.1 us
    all_to_all x5, blocking collectives: 81.5 us -> 79.8 us  [exchange(): lax.all_to_all(values, names, split_axis=0, concat_axis=0, tiled=True, ax...]
    all_to_all x1, waiting for transfers between devices: 0.02 us -> 1.72 us  [exchange(): lax.all_to_all(values, names, split_axis=0, concat_axis=0, tiled=True, ax...]
    all_to_all x1, starting transfers between devices: 11.5 us -> 10.2 us  [exchange(): lax.all_to_all(values, names, split_axis=0, concat_axis=0, tiled=True, ax...]
    all_gather x1, blocking collectives: 2.79 us -> 3.92 us  [per_device(): lax.all_gather(jnp.concatenate([features[:, k:k + 128] for k in range(0,...]
  transfers between devices with their start and end apart: 2 -> 2, of which waited for: 0 -> 1; matrix products, arithmetic and copies ran while one was open for 1% -> 1% of each run, Pallas kernels for 3% -> 3%
where the time goes in v5:
time: 112 us; the launch traced here: 111 us
  blocking collectives  83.7 us (75%)
  starting transfers between devices  14.1 us (13%)
  Pallas kernels  8.16 us (7%)
  local copies, waits for them, and re-layouts  2.44 us (2%)
  waiting for transfers between devices  1.72 us (2%)
    all_to_all x5, blocking collectives, exchange(): lax.all_to_all(values, names, split_axis=0, concat_axis=0, tiled=True, ax...  79.8 us
    all_to_all x1, starting transfers between devices, exchange(): lax.all_to_all(values, names, split_axis=0, concat_axis=0, tiled=True, ax...  10.2 us
    all_gather x1, blocking collectives, per_device(): lax.all_gather(jnp.concatenate([features[:, k:k + 128] for k in range(0,...  3.92 us
    ppermute x1, starting transfers between devices, per_device(): there = lax.ppermute(here, 'core', [(k, nc - 1 - k) for k in range(nc)])  3.88 us
  transfers between devices with their start and end apart: 2, of which 1 were waited for; matrix products, arithmetic and copies ran while one was open for 1% of the time, Pallas kernels for 3%

profile of v5, /device:TPU:1, one launch (start us, length us, event | category | flops | bytes accessed | tf_op | source)
XLA Modules:
  0.0 111.2 jit_solution(2398933936328182082)
XLA Ops:
  0.6 1.5 %shard_map.95 = (bf16[32,1408]{1,0:T(8,128)(2,1)S(1)}, f32[8,512]{1,0:T(8,128)S(1)}) custom-call(s32[1,2]{1,0:T(1,128)} %refs_0_.1, s32[1,96]{1,0:T(1,128)} %bitcast.41, bf16[96,256]{1,0:T(8,128)(2,1)} %refs_2_.1, bf16[64,384]{1,0:T(8,128)(2,1)} %bitcast.39, bf16[64,512]{1,0:T(8,128)(2,1)} %bitcast.38), custom_call_target="tpu_custom_call" | custom-call | tf_op jit(solution)/shard_map/pallas_call | solution.py:260
  2.2 23.1 %all_to_all.30 = bf16[16,2,1408]{2,1,0:T(2,128)(2,1)S(1)} all-to-all(bf16[16,2,1408]{2,1,0:T(2,128)(2,1)S(1)} %reshape.50), channel_id=1, replica_groups={{80,88,96,104,112,120,0,8,16,24,32,40,48,56,64,72},{81,89,97,105,113,12..., dimensions={0} | all-to-all | bytes 180224 | tf_op jit(solution)/shard_map/all_to_all | solution.py:33
  25.4 0.1 broadcast_in_dim.8
  25.4 15.7 %all_to_all.31 = bf16[16,32,640]{2,1,0:T(8,128)(2,1)S(1)} all-to-all(bf16[16,32,640]{2,1,0:T(8,128)(2,1)S(1)} %bitcast.33), channel_id=1, replica_groups={{258,386,2,130,259,387,3,131,256,384,0,128,257,385,1,129},{262,390,6,13..., dimensions={0} | all-to-all | bytes 1310720 | tf_op jit(solution)/shard_map/all_to_all | solution.py:33
  41.3 0.0 copy-start
  41.3 0.0 copy-start.1
  41.4 3.9 %all-gather = bf16[3968,128]{1,0:T(8,128)(2,1)S(1)} all-gather(bf16[1984,128]{1,0:T(8,128)(2,1)S(1)} %constant_dynamic-update-slice_fusion), channel_id=2, replica_groups=mesh['x'=4,'z'=16,'core'=2,'batch'=4] {'core'}, dimensions={0}, use_global_device_ids=true | all-gather | bytes 1523712 | tf_op jit(solution)/shard_map/all_gather | solution.py:313
  45.3 0.1 pad_add_fusion.place_ref
  45.4 1.7 %shard_map.96 = (bf16[256,768]{1,0:T(8,128)(2,1)S(1)}, bf16[512,256]{1,0:T(8,128)(2,1)S(1)}) custom-call(s32[2]{0:T(128)S(1)} %pad_add_fusion.place_ref, bf16[512,384]{1,0:T(8,128)(2,1)S(1)} %bitcast.28, bf16[448,128]{1,0:T(8,128)(2,1)S(1)} %pad_maximum_fusion.1.kept_ref, bf16[2,1984,128]{2,1,0:T(8,128)(2,1)S(1)} %bitcast.23, ...), custom_call_target="tpu_custom_call" | custom-call | tf_op jit(solution)/shard_map/pallas_call | solution.py:320
  47.1 11.1 %all_to_all.32 = bf16[8,32,768]{2,1,0:T(8,128)(2,1)S(1)} all-to-all(bf16[8,32,768]{2,1,0:T(8,128)(2,1)S(1)} %bitcast.32), channel_id=1, replica_groups={{256,384,0,128,260,388,4,132},{257,385,1,129,261,389,5,133},{258,386,2,..., dimensions={0} | all-to-all | bytes 786432 | tf_op jit(solution)/shard_map/all_to_all | solution.py:33
  58.2 0.1 reduce_sum.21
  58.2 0.6 reshape.55
  58.9 10.2 %all-to-all-start.3 = ((bf16[16,2,768]{2,1,0:T(2,128)(2,1)}), bf16[16,2,768]{2,1,0:T(2,128)(2,1)S(1)}, u32[]{:S(2)}, u32[]{:S(2)}) async-start(bf16[16,2,768]{2,1,0:T(2,128)(2,1)} %reshape.55), calls=%async_computation.3 | async-start | bytes 98304 | tf_op jit(solution)/shard_map/all_to_all | solution.py:33
  69.0 2.0 %shard_map.97 = (bf16[512,512]{1,0:T(8,128)(2,1)S(1)}, bf16[512,512]{1,0:T(8,128)(2,1)S(1)}) custom-call(s32[2]{0:T(128)S(1)} %pad_add_fusion.place_ref, bf16[512,384]{1,0:T(8,128)(2,1)S(1)} %bitcast.29, bf16[2,1984,128]{2,1,0:T(8,128)(2,1)S(1)} %bitcast.24, bf16[512,384]{1,0:T(8,128)(2,1)S(1)} %copy-done.1), custom_call_target="tpu_custom_call" | custom-call | tf_op jit(solution)/shard_map/pallas_call | solution.py:335
  71.0 0.0 copy-start.2
  71.0 0.8 copy-done.2
  71.8 1.7 %all-to-all-done.3 = bf16[16,2,768]{2,1,0:T(2,128)(2,1)S(1)} async-done(((bf16[16,2,768]{2,1,0:T(2,128)(2,1)}), bf16[16,2,768]{2,1,0:T(2,128)(2,1)S(1)}, u32[]{:S(2)}, u32[]{:S(2)}) %all-to-all-start.3) | async-done | bytes 49184 | tf_op jit(solution)/shard_map/all_to_all | solution.py:33
  73.6 14.2 %all_to_all.33 = bf16[16,2,768]{2,1,0:T(2,128)(2,1)S(1)} all-to-all(bf16[16,2,768]{2,1,0:T(2,128)(2,1)S(1)} %broadcast_in_dim.9), channel_id=1, replica_groups={{80,88,96,104,112,120,0,8,16,24,32,40,48,56,64,72},{81,89,97,105,113,12..., dimensions={0} | all-to-all | bytes 98304 | tf_op jit(solution)/shard_map/all_to_all | solution.py:33
  87.8 0.1 broadcast_in_dim.22
  87.9 15.8 %all_to_all.34 = bf16[16,32,768]{2,1,0:T(8,128)(2,1)S(1)} all-to-all(bf16[16,32,768]{2,1,0:T(8,128)(2,1)S(1)} %broadcast_in_dim.22), channel_id=1, replica_groups={{258,386,2,130,259,387,3,131,256,384,0,128,257,385,1,129},{262,390,6,13..., dimensions={0} | all-to-all | bytes 1572864 | tf_op jit(solution)/shard_map/all_to_all | solution.py:33
  103.7 3.9 %collective-permute-start = (bf16[512,768]{1,0:T(8,128)(2,1)S(1)}, bf16[512,768]{1,0:T(8,128)(2,1)S(1)}, u32[]{:S(2)}, u32[]{:S(2)}) collective-permute-start(bf16[512,768]{1,0:T(8,128)(2,1)S(1)} %bitcast.30), channel_id=1, source_target_pairs={{0,4},{4,0},{1,5},{5,1},{2,6},{6,2},{3,7},{7,3},{8,12},{12,8},{9,1... | collective-permute-start | bytes 2359304 | tf_op jit(solution)/shard_map/ppermute | solution.py:356
  107.6 1.5 %shard_map.98 = (f32[512,512]{1,0:T(8,128)S(1)}, f32[256,512]{1,0:T(8,128)S(1)}, f32[256,1]{1,0:T(8,128)S(1)}) custom-call(bf16[512,512]{1,0:T(8,128)(2,1)} %copy-done.2, f32[1,256]{1,0:T(1,128)} %bitcast.40, bf16[512,768]{1,0:T(8,128)(2,1)S(1)} %bitcast.31), custom_call_target="tpu_custom_call" | custom-call | tf_op jit(solution)/shard_map/pallas_call | solution.py:357
  109.1 0.6 constant_dynamic-slice_fusion
  109.7 1.5 %shard_map.99 = bf16[512,512]{1,0:T(8,128)(2,1)} custom-call(bf16[512,512]{1,0:T(8,128)(2,1)S(1)} %get-tuple-element.41.kernel_ref, bf16[512,768]{1,0:T(8,128)(2,1)S(1)} %collective-permute-done.there_ref, f32[512,512]{1,0:T(8,128)S(1)} %get-tuple-element.44.slope_ref, f32[256,512]{1,0:T(8,128)S(1)} %get-tuple-element.45.project_ref, ...), custom_call_target="tpu_custom_call" | custom-call | tf_op jit(solution)/shard_map/pallas_call | solution.py:378
  (27 shorter events, 0.4 us)
Async XLA Ops:
  41.3 4.0 %copy-start = (bf16[512,512]{1,0:T(8,128)(2,1)S(1)}, bf16[512,512]{1,0:T(8,128)(2,1)}, u32[]{:S(2)}) copy-start(bf16[512,512]{1,0:T(8,128)(2,1)} %weights_ref.3) | copy-start | bytes 1572868
  41.3 4.0 %copy-start.1 = (bf16[512,384]{1,0:T(8,128)(2,1)S(1)}, bf16[512,384]{1,0:T(8,128)(2,1)}, u32[]{:S(2)}) copy-start(bf16[512,384]{1,0:T(8,128)(2,1)} %centers_ref.3) | copy-start | bytes 1179652
  58.9 14.7 %all-to-all-start.3 = ((bf16[16,2,768]{2,1,0:T(2,128)(2,1)}), bf16[16,2,768]{2,1,0:T(2,128)(2,1)S(1)}, u32[]{:S(2)}, u32[]{:S(2)}) async-start(bf16[16,2,768]{2,1,0:T(2,128)(2,1)} %reshape.55), calls=%async_computation.3 | async-start | bytes 98304 | tf_op jit(solution)/shard_map/all_to_all | solution.py:33
  71.0 0.8 copy-start.2
  103.7 6.0 %collective-permute-start = (bf16[512,768]{1,0:T(8,128)(2,1)S(1)}, bf16[512,768]{1,0:T(8,128)(2,1)S(1)}, u32[]{:S(2)}, u32[]{:S(2)}) collective-permute-start(bf16[512,768]{1,0:T(8,128)(2,1)S(1)} %bitcast.30), channel_id=1, source_target_pairs={{0,4},{4,0},{1,5},{5,1},{2,6},{6,2},{3,7},{7,3},{8,12},{12,8},{9,1... | collective-permute-start | bytes 2359304 | tf_op jit(solution)/shard_map/ppermute | solution.py:356
